TPU v7x, 512 devices: a whole 4x4x16 slice. The times are simulated.
512 devices in a mesh: shard: 32 (over y_lo, z), rep: 16 (over x, y_hi, core).
Axes of the slice: x: 4, y: 4 (y_hi: 2, y_lo: 2; y = y_hi * 2 + y_lo), z: 16, core: 2. Of those that a mesh axis runs over, the one named last changes fastest.
Arguments:
- node_feat: bfloat16 [4096, 128, 256], P(('shard', 'rep'))
- node_cot: bfloat16 [4096, 128, 256], P(('shard', 'rep'))
- edge_length: float32 [4096, 1536], P(('shard', 'rep')), may hold values from 0.5 to 5.5
- atom_count: int32 [4096], P(('shard', 'rep')), may hold values from 32 to 128, as said below
- edge_count: int32 [4096], P(('shard', 'rep')), may hold values from 384 to 1536, as said below
- edge_source: int32 [4096, 1536], P(('shard', 'rep')), may hold values from 0 to 127, as said below
- edge_target: int32 [4096, 1536], P(('shard', 'rep')), may hold values from 0 to 127, as said below
- dataset_tag: int32 [4096], P(('shard', 'rep')), may hold values from 0 to 1
- charge_tag: int32 [4096], P(('shard', 'rep')), may hold values from 0 to 1
- spin_tag: int32 [4096], P(('shard', 'rep')), may hold values from 0 to 1
- dataset_gain: float32 [2, 32], replicated, may hold values from 0.2 to 5
- charge_gain: float32 [2, 32], replicated, may hold values from 0.2 to 5
- spin_gain: float32 [2, 32], replicated, may hold values from 0.2 to 5
- params: float32 [32, 128, 2, 128], P(None, 'shard'), may hold values from -0.375 to 0.375
- moment_one: float32 [32, 128, 2, 128], P(None, 'shard'), may hold values from -0.9 to 0.9
- moment_two: float32 [32, 128, 2, 128], P(None, 'shard'), may hold values from 0.0001 to 0.01
Outputs:
- new_params: float32 [32, 128, 2, 128], P(None, 'shard')
- new_moment_one: float32 [32, 128, 2, 128], P(None, 'shard')
- new_moment_two: float32 [32, 128, 2, 128], P(None, 'shard')
- full_weights: bfloat16 [32, 128, 2, 128], replicated
Inputs may be any that keep to these rules, and one draw needn't show every extreme that they name: `atom_count`: every system has at least a quarter of its atom slots filled. `edge_count`: every system has at least a quarter of its edge slots live. `edge_source`: every slot, live or not, names an atom below its system's atom count. `edge_target`: every slot, live or not, names an atom below its system's atom count.
All inputs are finite; a program needn't handle non-finite values.
Results may differ from a plain program's by a relative error of at most 0.0036.
Values may be sent and summed in bfloat16 or wider, within the bound.
No kernel may reach another device: no remote copies, remote signals or barrier semaphores. Data moves between devices by JAX's collectives and lax.ppermute only.
A program may use at most 64 MiB of HBM per device.

v0:
```python
import math

import jax
import jax.numpy as jnp
from jax import lax
from jax.sharding import PartitionSpec as P

STEP = 10


beta_one = 0.9
beta_two = 0.999
adam_eps = 1e-08
learn_rate = 0.01
decay_rate = 0.01
cutoff_radius = 6.0


def envelope(length):
    ratio = length / cutoff_radius
    return 1.0 - 21.0 * ratio**5 + 35.0 * ratio**6 - 15.0 * ratio**7


def mixing_table(dataset_gain, charge_gain, spin_gain):
    product_table = (
        dataset_gain[:, None, None, :] * charge_gain[None, :, None, :] * spin_gain[None, None, :, :]
    )
    product_table = product_table.reshape(-1, product_table.shape[-1])
    return product_table / jnp.sum(product_table, axis=1, keepdims=True)


def onehot_rows(dataset_tag, charge_tag, spin_tag, charge_count, spin_count, row_total):
    tag_rows = (dataset_tag * charge_count + charge_tag) * spin_count + spin_tag
    return (tag_rows[:, None] == jnp.arange(row_total, dtype=jnp.int32)[None, :]).astype(
        jnp.float32
    )


def select_rows(node_rows, slot_ids):
    atom_ids = lax.broadcasted_iota(jnp.int32, (1, node_rows.shape[0]), 1)
    selector = (slot_ids[:, None] == atom_ids).astype(jnp.bfloat16)
    return jnp.dot(selector, node_rows, preferred_element_type=jnp.float32)


def system_product(items):
    feat_rows, cot_rows, length_row, atoms_here, edges_here, source_row, target_row = items
    atom_slots = feat_rows.shape[0]
    edge_input = (select_rows(feat_rows, source_row) * envelope(length_row)[:, None]).astype(
        jnp.bfloat16
    )
    slot_index = lax.broadcasted_iota(jnp.int32, source_row.shape, 0)
    live_mask = (slot_index < edges_here).astype(jnp.float32)
    factor = live_mask * (float(atom_slots) / atoms_here.astype(jnp.float32))
    edge_grad = (select_rows(cot_rows, target_row) * factor[:, None]).astype(jnp.bfloat16)
    return lax.dot_general(
        edge_input, edge_grad, (((0,), (0,)), ((), ())), preferred_element_type=jnp.float32
    )


def adam_update(gradients, params, moment_one, moment_two, square_sum, norm_limit):
    clip_factor = jnp.minimum(1.0, norm_limit / (jnp.sqrt(square_sum) + 1e-06))
    clipped = clip_factor * gradients
    new_one = beta_one * moment_one + (1.0 - beta_one) * clipped
    new_two = beta_two * moment_two + (1.0 - beta_two) * clipped * clipped
    first_fix = 1.0 - beta_one**STEP
    second_fix = 1.0 - beta_two**STEP
    direction = new_one / first_fix / (jnp.sqrt(new_two / second_fix) + adam_eps)
    new_params = params - learn_rate * (direction + decay_rate * params)
    return (new_params, new_one, new_two)


def local(
    node_feat,
    node_cot,
    edge_length,
    atom_count,
    edge_count,
    edge_source,
    edge_target,
    dataset_tag,
    charge_tag,
    spin_tag,
    dataset_gain,
    charge_gain,
    spin_gain,
    params,
    moment_one,
    moment_two,
):
    channels = node_feat.shape[2] // 2
    mixing = mixing_table(dataset_gain, charge_gain, spin_gain)
    tag_onehot = onehot_rows(
        dataset_tag, charge_tag, spin_tag, charge_gain.shape[0], spin_gain.shape[0], mixing.shape[0]
    )
    products = lax.map(
        system_product,
        (node_feat, node_cot, edge_length, atom_count, edge_count, edge_source, edge_target),
    )
    real_part = products[:, :channels, :channels] + products[:, channels:, channels:]
    imag_part = products[:, :channels, channels:] - products[:, channels:, :channels]
    system_grad = jnp.stack([real_part, imag_part], axis=2)
    local_term = jnp.einsum(
        "sk,scto->ckto", tag_onehot, system_grad, precision=lax.Precision.HIGHEST
    )
    summed = lax.psum_scatter(local_term, "shard", scatter_dimension=0, tiled=True)
    summed = lax.psum(summed, "rep")
    gradients = jnp.einsum("ke,ckto->ecto", mixing, summed, precision=lax.Precision.HIGHEST)
    square_sum = lax.psum(jnp.sum(gradients * gradients), "shard")
    norm_limit = math.sqrt(mixing.shape[1] * 2 * channels * channels)
    new_params, new_one, new_two = adam_update(
        gradients, params, moment_one, moment_two, square_sum, norm_limit
    )
    full_weights = lax.all_gather(new_params.astype(jnp.bfloat16), "shard", axis=1, tiled=True)
    return (new_params, new_one, new_two, full_weights)


def solution(mesh):
    placed = (
        P(("shard", "rep"), None, None),
        P(("shard", "rep"), None, None),
        P(("shard", "rep"), None),
        P(("shard", "rep")),
        P(("shard", "rep")),
        P(("shard", "rep"), None),
        P(("shard", "rep"), None),
        P(("shard", "rep")),
        P(("shard", "rep")),
        P(("shard", "rep")),
        P(),
        P(),
        P(),
        P(None, "shard", None, None),
        P(None, "shard", None, None),
        P(None, "shard", None, None),
    )
    return jax.shard_map(
        local,
        mesh=mesh,
        in_specs=placed,
        out_specs=(
            P(None, "shard", None, None),
            P(None, "shard", None, None),
            P(None, "shard", None, None),
            P(),
        ),
        check_vma=False,
    )
```

profile of v0, /device:TPU:2, one launch (start us, length us, event | category | flops | bytes accessed | tf_op | source)
XLA Modules:
  0.0 490.4 jit_solution(9929910309225051668)
XLA Ops:
  7.2 75.9 %while.10 = (s32[]{:T(128)}, f32[8,256,256]{2,1,0:T(8,128)S(1)}, s32[8,1536]{1,0:T(8,128)}, bf16[8,128,256]{2,1,0:T(8,128)(2,1)}, f32[8,1536]{1,0:T(8,128)}, /*i...) while((s32[]{:T(128)}, f32[8,256,256]{2,1,0:T(8,128)S(1)}, ...), condition=%wide.region_2.3_spmd, body=%wide.region_1.2_spmd.sunk | while | flops 404642304 | bytes 2051753 | solution.py:95
  8.9 2.2 fusion.52
  15.0 1.7 fusion.54
  18.4 2.2 fusion.52
  24.5 1.7 fusion.54
  27.9 2.2 fusion.52
  34.0 1.7 fusion.54
  37.4 2.2 fusion.52
  43.5 1.7 fusion.54
  46.9 2.2 fusion.52
  52.9 1.7 fusion.54
  56.4 2.2 fusion.52
  62.4 1.7 fusion.54
  65.9 2.2 fusion.52
  71.9 1.7 fusion.54
  75.4 2.2 fusion.52
  79.5 1.2 dynamic_slice.48
  81.4 1.7 fusion.54
  83.9 2.2 convolution_bitcast_fusion
  86.4 142.3 %reduce-scatter.2.cloned.1.call-done = f32[4,8,2,128]{3,1,2,0:T(8,128)} async-done(((f32[128,8,2,128]{3,1,2,0:T(8,128)}), f32[4,8,2,128]{3,1,2,0:T(8,128)}) %reduce-scatter.2.cloned.1.call-update) | async-done | bytes 32784 | tf_op jit(solution)/shard_map/reduce_scatter | solution.py:105
  228.7 57.3 %psum.14 = f32[4,8,2,128]{3,1,2,0:T(8,128)S(1)} all-reduce(f32[4,8,2,128]{3,1,2,0:T(8,128)} %reduce-scatter.2.cloned.1.call-done), channel_id=1, replica_groups=mesh['shard'=32,'rep'=16] {'rep'}, use_global_device_ids=true, to_apply=%region_4.5 | all-reduce | flops 8192 | bytes 65536 | tf_op jit(solution)/shard_map/psum | solution.py:106
  286.9 61.9 %psum.15 = f32[]{:T(128)} all-reduce(f32[]{:T(128)} %get-tuple-element.88), channel_id=1, replica_groups=mesh['shard'=32,'rep'=16] {'shard'}, use_global_device_ids=true, to_apply=%region_6.7 | all-reduce | flops 1 | bytes 8 | tf_op jit(solution)/shard_map/psum | solution.py:108
  352.7 125.8 %all-gather.2.cloned.1.call-done = bf16[32,128,2,128]{3,0,2,1:T(8,128)(2,1)} async-done(((bf16[32,4,2,128]{3,0,2,1:T(8,128)(2,1)}), bf16[32,128,2,128]{3,0,2,1:T(8,128)(2,1)}) %all-gather.2.cloned.1.call-update) | async-done | bytes 2097168 | tf_op jit(solution)/shard_map/all_gather | solution.py:113
  478.5 5.1 %copy.35 = bf16[32,128,2,128]{3,2,1,0:T(2,128)(2,1)} copy(bf16[32,128,2,128]{3,0,2,1:T(8,128)(2,1)} %all-gather.2.cloned.1.call-done) | data formatting | bytes 4194304
  (81 shorter events, 42.5 us)
Async XLA Ops:
  7.2 221.5 %reduce-scatter.2.cloned.1.call-start = ((), (), s32[]{:S(2)}) async-start(), calls=%async_computation.1 | async-start | bytes 1081344 | tf_op jit(solution)/shard_map/reduce_scatter | solution.py:105
  83.2 0.7 copy-start.6
  83.2 0.7 copy-start.7
  83.2 0.7 copy-start.8
  83.9 2.3 copy-start.4
  83.9 2.3 copy-start.5
  83.9 2.4 copy-start.3
  83.9 265.7 %copy-start = (f32[32,4,2,128]{3,2,1,0:T(2,128)S(1)}, f32[32,4,2,128]{3,2,1,0:T(2,128)}, u32[]{:S(2)}) copy-start(f32[32,4,2,128]{3,2,1,0:T(2,128)} %param.31) | copy-start | bytes 393220
  83.9 265.7 %copy-start.1 = (f32[32,4,2,128]{3,2,1,0:T(2,128)S(1)}, f32[32,4,2,128]{3,2,1,0:T(2,128)}, u32[]{:S(2)}) copy-start(f32[32,4,2,128]{3,2,1,0:T(2,128)} %param.32) | copy-start | bytes 393220
  83.9 265.7 %copy-start.2 = (f32[32,4,2,128]{3,2,1,0:T(2,128)S(1)}, f32[32,4,2,128]{3,2,1,0:T(2,128)}, u32[]{:S(2)}) copy-start(f32[32,4,2,128]{3,2,1,0:T(2,128)} %param.33) | copy-start | bytes 393220
  86.1 392.3 %all-gather.2.cloned.1.call-start = ((), (), s32[]{:S(2)}) async-start(), calls=%async_computation.2 | async-start | bytes 2162688 | tf_op jit(solution)/shard_map/all_gather | solution.py:113
Sparse Core Ops, SparseCore 0:
  86.3 142.3 reduce-scatter.1
  350.5 127.8 all-gather.1
where the time goes:
time: 493 us; the launch traced here: 490 us
  waiting for transfers between devices  268 us (54%)
  blocking collectives  119 us (24%)
  local copies, waits for them, and re-layouts  34.8 us (7%)
  matrix products  34.5 us (7%)
  between operations  14.9 us (3%)
  other arithmetic  13 us (3%)
  loops' own time  5.91 us (1%)
    reduce_scatter x1, waiting for transfers between devices, local(): lax.psum_scatter(local_term, 'shard', scatter_dimension=0, tiled=True)  142 us
    all_gather x1, waiting for transfers between devices, local(): lax.all_gather(new_params.astype(jnp.bfloat16), 'shard', axis=1, tiled=True)  126 us
    psum x1, blocking collectives, local(): square_sum = lax.psum(jnp.sum(gradients * gradients), 'shard')  61.9 us
    psum x1, blocking collectives, local(): summed = lax.psum(summed, 'rep')  57.3 us
    dynamic_slice x24, local copies, waits for them, and re-layouts, local(): lax.map(system_product, (node_feat, node_cot, edge_length, atom_count, ed...  26.8 us
    dot_general x8, matrix products, select_rows(): return jnp.dot(selector, node_rows, preferred_element_type=jnp.float32)  17.5 us
    dot_general x8, matrix products, system_product(): lax.dot_general(edge_input, edge_grad, (((0,), (0,)), ((), ())), preferre...  13.8 us
  transfers between devices with their start and end apart: 2, of which 2 were waited for; matrix products, arithmetic and copies ran while one was open for 0% of the time, Pallas kernels for 0%

commit v1 on v0

v1 whole, which is shorter than its diff:
```python
import functools
import math

import jax
import jax.numpy as jnp
from jax import lax
from jax.experimental import pallas as pl
from jax.experimental.pallas import tpu as pltpu
from jax.sharding import PartitionSpec as P

STEP = 10

beta_one = 0.9
beta_two = 0.999
adam_eps = 1e-08
learn_rate = 0.01
decay_rate = 0.01
cutoff_radius = 6.0

EDGE_BLOCK = 512


def envelope(length):
    ratio = length / cutoff_radius
    return 1.0 - 21.0 * ratio**5 + 35.0 * ratio**6 - 15.0 * ratio**7


def grouped_kernel(
    data_tag,
    charge_tag,
    spin_tag,
    atoms_ref,
    edges_ref,
    feat_ref,
    cot_ref,
    length_ref,
    source_ref,
    target_ref,
    out_ref,
    total,
    product,
):
    system = pl.program_id(0)
    atom_slots, width = feat_ref.shape[1:]
    channels = width // 2
    slots = length_ref.shape[1]

    @pl.when(system == 0)
    def _():
        total[...] = jnp.zeros_like(total)

    feat = feat_ref[0].T
    cot = cot_ref[0].T
    edges_here = edges_ref[system]
    weight = jnp.full((1, EDGE_BLOCK), float(atom_slots), jnp.float32) / jnp.full(
        (1, EDGE_BLOCK), atoms_ref[system], jnp.int32
    ).astype(jnp.float32)
    atom_ids = lax.broadcasted_iota(jnp.int32, (atom_slots, EDGE_BLOCK), 0)
    slot_ids = lax.broadcasted_iota(jnp.int32, (1, EDGE_BLOCK), 1)
    row = pl.ds(system, 1)

    for block in range(slots // EDGE_BLOCK):
        first = block * EDGE_BLOCK

        def step(first=first, block=block):
            cols = pl.ds(first, EDGE_BLOCK)
            pick_source = (atom_ids == source_ref[row, cols]).astype(jnp.float32).astype(jnp.bfloat16)
            pick_target = (atom_ids == target_ref[row, cols]).astype(jnp.float32).astype(jnp.bfloat16)
            edge_input = jnp.dot(feat, pick_source, preferred_element_type=jnp.float32)
            edge_input = (edge_input * envelope(length_ref[row, cols])).astype(jnp.bfloat16)
            factor = jnp.where(slot_ids + first < edges_here, weight, 0.0)
            edge_grad = jnp.dot(cot, pick_target, preferred_element_type=jnp.float32)
            edge_grad = (edge_grad * factor).astype(jnp.bfloat16)
            part = lax.dot_general(
                edge_input,
                edge_grad,
                (((1,), (1,)), ((), ())),
                preferred_element_type=jnp.float32,
            )
            if block == 0:
                product[...] = part
            else:
                product[...] += part

        if block == 0:
            step()
        else:
            pl.when(first < edges_here)(step)

    tag = (data_tag[system] * 2 + charge_tag[system]) * 2 + spin_tag[system]
    total[2 * tag] += product[:channels, :channels] + product[channels:, channels:]
    total[2 * tag + 1] += product[:channels, channels:] - product[channels:, :channels]

    @pl.when(system == pl.num_programs(0) - 1)
    def _():
        out_ref[...] = total[...].astype(out_ref.dtype)


def grouped_sums(feat, cot, length, atoms, edges, source, target, data_tag, charge_tag, spin_tag):
    systems, atom_slots, width = feat.shape
    channels = width // 2
    slots = length.shape[1]
    whole = lambda i, *_: (0, 0)
    each = lambda i, *_: (i, 0, 0)
    return pl.pallas_call(
        grouped_kernel,
        out_shape=jax.ShapeDtypeStruct((16, channels, channels), jnp.bfloat16),
        grid_spec=pltpu.PrefetchScalarGridSpec(
            num_scalar_prefetch=5,
            grid=(systems,),
            in_specs=[
                pl.BlockSpec((1, atom_slots, width), each),
                pl.BlockSpec((1, atom_slots, width), each),
                pl.BlockSpec((systems, slots), whole),
                pl.BlockSpec((systems, slots), whole),
                pl.BlockSpec((systems, slots), whole),
            ],
            out_specs=pl.BlockSpec((16, channels, channels), lambda i, *_: (0, 0, 0)),
            scratch_shapes=[
                pltpu.VMEM((16, channels, channels), jnp.float32),
                pltpu.VMEM((width, width), jnp.float32),
            ],
        ),
        name="grouped_sums",
    )(data_tag, charge_tag, spin_tag, atoms, edges, feat, cot, length, source, target)


def expert_kernel(data_ref, charge_ref, spin_ref, sums_ref, grad_ref, square_ref):
    data_gain, charge_gain, spin_gain = data_ref[...], charge_ref[...], spin_ref[...]
    table = jnp.concatenate(
        [
            data_gain[d : d + 1] * charge_gain[c : c + 1] * spin_gain[s : s + 1]
            for d in range(2)
            for c in range(2)
            for s in range(2)
        ],
        axis=0,
    )
    mixing = table / jnp.sum(table, axis=1, keepdims=True)
    squares = None
    for channel in range(4):
        for part in range(2):
            rows = sums_ref[:, part, channel, :]
            grad = lax.dot_general(
                mixing,
                rows,
                (((0,), (0,)), ((), ())),
                precision=lax.Precision.HIGHEST,
                preferred_element_type=jnp.float32,
            )
            grad_ref[:, 2 * channel + part, :] = grad
            term = jnp.sum(grad * grad, axis=0, keepdims=True)
            squares = term if squares is None else squares + term
    square_ref[...] = jnp.broadcast_to(squares[None], square_ref.shape)


def expert_grads(data_gain, charge_gain, spin_gain, sums, shards):
    experts = data_gain.shape[1]
    return pl.pallas_call(
        expert_kernel,
        out_shape=(
            jax.ShapeDtypeStruct((experts, 8, 128), jnp.float32),
            jax.ShapeDtypeStruct((shards, 1, 128), jnp.float32),
        ),
        name="expert_grads",
    )(data_gain, charge_gain, spin_gain, sums)


def adam_kernel(
    norm_limit,
    first_ref,
    square_ref,
    grad_ref,
    params_ref,
    one_ref,
    two_ref,
    new_params_ref,
    new_one_ref,
    new_two_ref,
    share_ref,
):
    squares = jnp.sum(square_ref[...], axis=0)
    square_sum = jnp.sum(squares, axis=1, keepdims=True)
    clip_factor = jnp.minimum(1.0, norm_limit / (jnp.sqrt(square_sum) + 1e-06))
    clipped = clip_factor[None] * grad_ref[...]
    new_one = beta_one * one_ref[...] + (1.0 - beta_one) * clipped
    new_two = beta_two * two_ref[...] + (1.0 - beta_two) * clipped * clipped
    first_fix = 1.0 - beta_one**STEP
    second_fix = 1.0 - beta_two**STEP
    direction = new_one / first_fix / (jnp.sqrt(new_two / second_fix) + adam_eps)
    params = params_ref[...]
    new_params_ref[...] = params - learn_rate * (direction + decay_rate * params)
    new_one_ref[...] = new_one
    new_two_ref[...] = new_two
    mine = new_params_ref[pl.ds(first_ref[0], 2)].reshape(16, 128).astype(jnp.bfloat16)
    share_ref[...] = jnp.broadcast_to(mine[None], share_ref.shape)


def adam_update(first, squares, grads, params, moment_one, moment_two, norm_limit):
    shards = squares.shape[0]
    state = jax.ShapeDtypeStruct(params.shape, jnp.float32)
    vmem = pl.BlockSpec(memory_space=pltpu.VMEM)
    return pl.pallas_call(
        functools.partial(adam_kernel, norm_limit),
        out_shape=(state, state, state, jax.ShapeDtypeStruct((shards, 16, 128), jnp.bfloat16)),
        in_specs=[pl.BlockSpec(memory_space=pltpu.SMEM)] + [vmem] * 5,
        out_specs=(vmem,) * 4,
        name="adam_update",
    )(first, squares, grads, params, moment_one, moment_two)


def exchange(array, axis, groups=None):
    return lax.all_to_all(array, axis, 0, 0, axis_index_groups=groups, tiled=True)


def local(
    node_feat,
    node_cot,
    edge_length,
    atom_count,
    edge_count,
    edge_source,
    edge_target,
    dataset_tag,
    charge_tag,
    spin_tag,
    dataset_gain,
    charge_gain,
    spin_gain,
    params,
    moment_one,
    moment_two,
):
    channels = node_feat.shape[2] // 2
    shards, reps = 32, 16
    experts, own = params.shape[:2]
    shape = params.shape
    rows = (experts, own * 2, channels)
    place = lax.axis_index("rep")
    first = jnp.bitwise_and(place, 1) * (experts // 2) + jnp.bitwise_and(place, reps - 2)

    sums = grouped_sums(
        node_feat,
        node_cot,
        edge_length,
        atom_count,
        edge_count,
        edge_source,
        edge_target,
        dataset_tag,
        charge_tag,
        spin_tag,
    )
    sums = exchange(sums, "rep")
    sums = jnp.sum(sums.astype(jnp.float32), axis=0).reshape(shards, own, channels)
    sums = exchange(sums, "shard")
    sums = jnp.sum(sums, axis=0)
    sums = exchange(jnp.broadcast_to(sums[None], (reps, own, channels)), "rep")
    grads, squares = expert_grads(
        dataset_gain, charge_gain, spin_gain, sums.reshape(8, 2, own, channels), shards
    )
    squares = exchange(squares, "shard")
    norm_limit = math.sqrt(experts * 2 * channels * channels)
    new_params, new_one, new_two, share = adam_update(
        first.reshape(1),
        squares,
        grads,
        params.reshape(rows),
        moment_one.reshape(rows),
        moment_two.reshape(rows),
        norm_limit,
    )
    share = exchange(share, "shard").reshape(shards, 2, own * 2, channels)
    share = jnp.broadcast_to(jnp.swapaxes(share, 0, 1)[None], (8, 2, shards, own * 2, channels))
    share = exchange(share, "rep", [[2 * i + core for i in range(8)] for core in range(2)])
    share = jnp.broadcast_to(share[None], (2,) + share.shape)
    share = exchange(share, "rep", [[2 * i, 2 * i + 1] for i in range(8)])
    full_weights = share.reshape(experts, shards * own, 2, channels)
    return (new_params.reshape(shape), new_one.reshape(shape), new_two.reshape(shape), full_weights)


def solution(mesh):
    placed = (
        P(("shard", "rep"), None, None),
        P(("shard", "rep"), None, None),
        P(("shard", "rep"), None),
        P(("shard", "rep")),
        P(("shard", "rep")),
        P(("shard", "rep"), None),
        P(("shard", "rep"), None),
        P(("shard", "rep")),
        P(("shard", "rep")),
        P(("shard", "rep")),
        P(),
        P(),
        P(),
        P(None, "shard", None, None),
        P(None, "shard", None, None),
        P(None, "shard", None, None),
    )
    return jax.shard_map(
        local,
        mesh=mesh,
        in_specs=placed,
        out_specs=(
            P(None, "shard", None, None),
            P(None, "shard", None, None),
            P(None, "shard", None, None),
            P(),
        ),
        check_vma=False,
    )
```

time: 493 us -> 144 us (0.29)
  the two profiles are of different devices: /device:TPU:2 before, /device:TPU:1 now
where the time goes in v1:
time: 144 us
  blocking collectives  107 us (74%)
  Pallas kernels  17.1 us (12%)
  waiting for transfers between devices  12.1 us (8%)
  starting transfers between devices  3.83 us (3%)
  local copies, waits for them, and re-layouts  2.72 us (2%)
    all_to_all x6, blocking collectives, exchange(): lax.all_to_all(array, axis, 0, 0, axis_index_groups=groups, tiled=True)  107 us
    pallas_call x1, Pallas kernels, grouped_sums(): pl.pallas_call(grouped_kernel, out_shape=jax.ShapeDtypeStruct((16, channe...  13.1 us
    all_to_all x1, waiting for transfers between devices, exchange(): lax.all_to_all(array, axis, 0, 0, axis_index_groups=groups, tiled=True)  12.1 us
    all_to_all x1, starting transfers between devices, exchange(): lax.all_to_all(array, axis, 0, 0, axis_index_groups=groups, tiled=True)  3.83 us
  transfers between devices with their start and end apart: 1, of which 1 were waited for; matrix products, arithmetic and copies ran while one was open for 0% of the time, Pallas kernels for 0%

profile of v1, /device:TPU:1, one launch (start us, length us, event | category | flops | bytes accessed | tf_op | source)
XLA Modules:
  0.0 143.6 jit_solution(1245035407072124494)
XLA Ops:
  0.6 13.1 %grouped_sums.1 = bf16[16,128,128]{2,1,0:T(8,128)(2,1)} custom-call(s32[8]{0:T(128)} %data_tag.1, s32[8]{0:T(128)} %charge_tag.1, s32[8]{0:T(128)} %spin_tag.1, s32[8]{0:T(128)} %atoms_ref.1, s32[8]{0:T(128)} %edges_ref.1, bf16[8,128,256]{2,1,0:T(8,128)(2,1)} %feat_ref.1, bf16[8,128,256]{2,1,0:T(8,128)(2,1)} %cot_ref.1, f32[8,1536]{1,0:T(8,128)} %length_ref.1, ...), custom_call_target="tpu_custom_call" | custom-call | tf_op jit(solution)/shard_map/grouped_sums/pallas_call | solution.py:105
  13.7 22.3 %all_to_all.35 = bf16[16,128,128]{2,1,0:T(8,128)(2,1)S(1)} all-to-all(bf16[16,128,128]{2,1,0:T(8,128)(2,1)} %grouped_sums.1), channel_id=1, replica_groups=mesh['shard'=32,'rep'=16] {'rep'}, dimensions={0} | all-to-all | bytes 1048576 | tf_op jit(solution)/shard_map/all_to_all | solution.py:213
  36.0 0.1 convert_reduce_fusion
  36.1 27.8 %all_to_all.36 = f32[32,4,128]{2,1,0:T(4,128)S(1)} all-to-all(f32[32,4,128]{2,1,0:T(4,128)S(1)} %bitcast.15), channel_id=1, replica_groups=mesh['shard'=32,'rep'=16] {'shard'}, dimensions={0} | all-to-all | bytes 131072 | tf_op jit(solution)/shard_map/all_to_all | solution.py:213
  63.9 12.9 %all_to_all.37 = f32[16,4,128]{2,1,0:T(4,128)} all-to-all(f32[16,4,128]{2,1,0:T(4,128)S(1)} %broadcast_in_dim.6), channel_id=1, replica_groups=mesh['shard'=32,'rep'=16] {'rep'}, dimensions={0} | all-to-all | bytes 65536 | tf_op jit(solution)/shard_map/all_to_all | solution.py:213
  76.8 1.9 %expert_grads.1 = (f32[32,8,128]{2,1,0:T(8,128)}, f32[32,1,128]{2,1,0:T(1,128)}) custom-call(f32[2,32]{1,0:T(2,128)} %data_ref.1, f32[2,32]{1,0:T(2,128)} %charge_ref.1, f32[2,32]{1,0:T(2,128)} %spin_ref.1, f32[8,2,4,128]{3,2,1,0:T(4,128)} %bitcast.19), custom_call_target="tpu_custom_call" | custom-call | tf_op jit(solution)/shard_map/expert_grads/pallas_call | solution.py:159
  78.8 3.8 %all-to-all-start.3 = ((f32[32,1,128]{2,1,0:T(1,128)}), f32[32,1,128]{2,1,0:T(1,128)S(1)}, u32[]{:S(2)}, u32[]{:S(2)}) async-start(f32[32,1,128]{2,1,0:T(1,128)} %get-tuple-element.10), calls=%async_computation.3 | async-start | bytes 32768 | tf_op jit(solution)/shard_map/all_to_all | solution.py:213
  82.6 12.1 %all-to-all-done.3.square_ref = f32[32,1,128]{2,1,0:T(1,128)S(1)} async-done(((f32[32,1,128]{2,1,0:T(1,128)}), f32[32,1,128]{2,1,0:T(1,128)S(1)}, u32[]{:S(2)}, u32[]{:S(2)}) %all-to-all-start.3) | async-done | bytes 16416 | tf_op jit(solution)/shard_map/all_to_all | solution.py:213
  94.8 0.0 copy-start
  94.8 0.6 copy-done
  95.3 2.1 %adam_update.1 = (f32[32,8,128]{2,1,0:T(8,128)}, f32[32,8,128]{2,1,0:T(8,128)}, f32[32,8,128]{2,1,0:T(8,128)}, bf16[32,16,128]{2,1,0:T(8,128)(2,1)}) custom-call(s32[1]{0:T(128)} %bitcast.first_ref, f32[32,1,128]{2,1,0:T(1,128)} %copy-done, f32[32,8,128]{2,1,0:T(8,128)} %get-tuple-element.11.grad_ref, f32[32,8,128]{2,1,0:T(8,128)} %bitcast.16, ...), custom_call_target="tpu_custom_call" | custom-call | tf_op jit(solution)/shard_map/adam_update/pallas_call | solution.py:203
  97.4 18.7 %all_to_all.38 = bf16[32,16,128]{2,1,0:T(8,128)(2,1)S(1)} all-to-all(bf16[32,16,128]{2,1,0:T(8,128)(2,1)} %get-tuple-element.15), channel_id=1, replica_groups=mesh['shard'=32,'rep'=16] {'shard'}, dimensions={0} | all-to-all | bytes 262144 | tf_op jit(solution)/shard_map/all_to_all | solution.py:213
  116.2 0.2 broadcast_in_dim.7
  116.4 16.4 %all_to_all.39 = bf16[8,2,32,8,128]{4,3,2,1,0:T(8,128)(2,1)S(1)} all-to-all(bf16[8,2,32,8,128]{4,3,2,1,0:T(8,128)(2,1)S(1)} %broadcast_in_dim.7), channel_id=1, replica_groups={{0,2,4,6,8,10,12,14},{1,3,5,7,9,11,13,15},{16,18,20,22,24,26,28,30},{17..., dimensions={0} | all-to-all | bytes 2097152 | tf_op jit(solution)/shard_map/all_to_all | solution.py:213
  132.8 0.6 broadcast_in_dim.8
  133.4 8.9 %all_to_all.40 = bf16[2,8,2,32,8,128]{5,4,3,2,1,0:T(8,128)(2,1)S(1)} all-to-all(bf16[2,8,2,32,8,128]{5,4,3,2,1,0:T(8,128)(2,1)S(1)} %broadcast_in_dim.8), channel_id=1, replica_groups={{0,1},{2,3},{4,5},{6,7},{8,9},{10,11},{12,13},{14,15},{16,17},{18,19},{..., dimensions={0} | all-to-all | bytes 4194304 | tf_op jit(solution)/shard_map/all_to_all | solution.py:213
  142.2 1.3 copy.26
  (3 shorter events, 0.1 us)
Async XLA Ops:
  78.8 16.0 %all-to-all-start.3 = ((f32[32,1,128]{2,1,0:T(1,128)}), f32[32,1,128]{2,1,0:T(1,128)S(1)}, u32[]{:S(2)}, u32[]{:S(2)}) async-start(f32[32,1,128]{2,1,0:T(1,128)} %get-tuple-element.10), calls=%async_computation.3 | async-start | bytes 32768 | tf_op jit(solution)/shard_map/all_to_all | solution.py:213
  94.8 0.6 copy-start

commit v2 on v1

--- a/solution.py
+++ b/solution.py
@@ -17,7 +17,8 @@
 decay_rate = 0.01
 cutoff_radius = 6.0
 
-EDGE_BLOCK = 512
+HELD = 4
+PARAMS = pltpu.CompilerParams(vmem_limit_bytes=24 * 2**20)
 
 
 def envelope(length):
@@ -38,60 +39,44 @@
     target_ref,
     out_ref,
     total,
-    product,
 ):
-    system = pl.program_id(0)
-    atom_slots, width = feat_ref.shape[1:]
+    step = pl.program_id(0)
+    held, atom_slots, width = feat_ref.shape
     channels = width // 2
     slots = length_ref.shape[1]
 
-    @pl.when(system == 0)
+    @pl.when(step == 0)
     def _():
         total[...] = jnp.zeros_like(total)
 
-    feat = feat_ref[0].T
-    cot = cot_ref[0].T
-    edges_here = edges_ref[system]
-    weight = jnp.full((1, EDGE_BLOCK), float(atom_slots), jnp.float32) / jnp.full(
-        (1, EDGE_BLOCK), atoms_ref[system], jnp.int32
-    ).astype(jnp.float32)
-    atom_ids = lax.broadcasted_iota(jnp.int32, (atom_slots, EDGE_BLOCK), 0)
-    slot_ids = lax.broadcasted_iota(jnp.int32, (1, EDGE_BLOCK), 1)
-    row = pl.ds(system, 1)
-
-    for block in range(slots // EDGE_BLOCK):
-        first = block * EDGE_BLOCK
-
-        def step(first=first, block=block):
-            cols = pl.ds(first, EDGE_BLOCK)
-            pick_source = (atom_ids == source_ref[row, cols]).astype(jnp.float32).astype(jnp.bfloat16)
-            pick_target = (atom_ids == target_ref[row, cols]).astype(jnp.float32).astype(jnp.bfloat16)
-            edge_input = jnp.dot(feat, pick_source, preferred_element_type=jnp.float32)
-            edge_input = (edge_input * envelope(length_ref[row, cols])).astype(jnp.bfloat16)
-            factor = jnp.where(slot_ids + first < edges_here, weight, 0.0)
-            edge_grad = jnp.dot(cot, pick_target, preferred_element_type=jnp.float32)
-            edge_grad = (edge_grad * factor).astype(jnp.bfloat16)
-            part = lax.dot_general(
-                edge_input,
-                edge_grad,
-                (((1,), (1,)), ((), ())),
-                preferred_element_type=jnp.float32,
-            )
-            if block == 0:
-                product[...] = part
-            else:
-                product[...] += part
-
-        if block == 0:
-            step()
-        else:
-            pl.when(first < edges_here)(step)
-
-    tag = (data_tag[system] * 2 + charge_tag[system]) * 2 + spin_tag[system]
-    total[2 * tag] += product[:channels, :channels] + product[channels:, channels:]
-    total[2 * tag + 1] += product[:channels, channels:] - product[channels:, :channels]
-
-    @pl.when(system == pl.num_programs(0) - 1)
+    atom_ids = lax.broadcasted_iota(jnp.int32, (atom_slots, slots), 0)
+    atom_ids = atom_ids.astype(jnp.float32).astype(jnp.bfloat16)
+    zero = jnp.zeros((atom_slots, slots), jnp.bfloat16)
+    one = jnp.ones((atom_slots, slots), jnp.bfloat16)
+    slot_ids = lax.broadcasted_iota(jnp.int32, (1, slots), 1)
+    for index in range(held):
+        system = step * held + index
+        row = pl.ds(system, 1)
+        atoms_here = jnp.full((1, slots), atoms_ref[system], jnp.int32).astype(jnp.float32)
+        weight = envelope(length_ref[row, :]) * (float(atom_slots) / atoms_here)
+        weight = jnp.where(slot_ids < edges_ref[system], weight, 0.0).astype(jnp.bfloat16)
+        source = source_ref[row, :].astype(jnp.float32).astype(jnp.bfloat16)
+        target = target_ref[row, :].astype(jnp.float32).astype(jnp.bfloat16)
+        links = lax.dot_general(
+            jnp.where(atom_ids == source, weight, zero),
+            jnp.where(atom_ids == target, one, zero),
+            (((1,), (1,)), ((), ())),
+            preferred_element_type=jnp.float32,
+        ).astype(jnp.bfloat16)
+        mixed = jnp.dot(links, cot_ref[index], preferred_element_type=jnp.float32)
+        product = jnp.dot(
+            feat_ref[index].T, mixed.astype(jnp.bfloat16), preferred_element_type=jnp.float32
+        )
+        tag = (data_tag[system] * 2 + charge_tag[system]) * 2 + spin_tag[system]
+        total[2 * tag] += product[:channels, :channels] + product[channels:, channels:]
+        total[2 * tag + 1] += product[:channels, channels:] - product[channels:, :channels]
+
+    @pl.when(step == pl.num_programs(0) - 1)
     def _():
         out_ref[...] = total[...].astype(out_ref.dtype)
 
@@ -107,19 +92,16 @@
         out_shape=jax.ShapeDtypeStruct((16, channels, channels), jnp.bfloat16),
         grid_spec=pltpu.PrefetchScalarGridSpec(
             num_scalar_prefetch=5,
-            grid=(systems,),
+            grid=(systems // HELD,),
             in_specs=[
-                pl.BlockSpec((1, atom_slots, width), each),
-                pl.BlockSpec((1, atom_slots, width), each),
+                pl.BlockSpec((HELD, atom_slots, width), each),
+                pl.BlockSpec((HELD, atom_slots, width), each),
                 pl.BlockSpec((systems, slots), whole),
                 pl.BlockSpec((systems, slots), whole),
                 pl.BlockSpec((systems, slots), whole),
             ],
             out_specs=pl.BlockSpec((16, channels, channels), lambda i, *_: (0, 0, 0)),
-            scratch_shapes=[
-                pltpu.VMEM((16, channels, channels), jnp.float32),
-                pltpu.VMEM((width, width), jnp.float32),
-            ],
+            scratch_shapes=[pltpu.VMEM((16, channels, channels), jnp.float32)],
         ),
         name="grouped_sums",
     )(data_tag, charge_tag, spin_tag, atoms, edges, feat, cot, length, source, target)
@@ -162,6 +144,7 @@
             jax.ShapeDtypeStruct((experts, 8, 128), jnp.float32),
             jax.ShapeDtypeStruct((shards, 1, 128), jnp.float32),
         ),
+        compiler_params=PARAMS,
         name="expert_grads",
     )(data_gain, charge_gain, spin_gain, sums)
 
@@ -205,6 +188,7 @@
         out_shape=(state, state, state, jax.ShapeDtypeStruct((shards, 16, 128), jnp.bfloat16)),
         in_specs=[pl.BlockSpec(memory_space=pltpu.SMEM)] + [vmem] * 5,
         out_specs=(vmem,) * 4,
+        compiler_params=PARAMS,
         name="adam_update",
     )(first, squares, grads, params, moment_one, moment_two)
 

time: 144 us -> 132 us (0.917)
  Pallas kernels: 17.1 us -> 8.63 us
  blocking collectives: 107 us -> 104 us
    pallas_call x1, Pallas kernels: 13.1 us -> 6.61 us  [grouped_sums(): pl.pallas_call(grouped_kernel, out_shape=jax.ShapeDtypeStruct((16, channe...]
    all_to_all x6, blocking collectives: 107 us -> 104 us  [exchange(): lax.all_to_all(array, axis, 0, 0, axis_index_groups=groups, tiled=True)]
where the time goes in v2:
time: 132 us
  blocking collectives  104 us (79%)
  waiting for transfers between devices  12.1 us (9%)
  Pallas kernels  8.63 us (7%)
  starting transfers between devices  3.83 us (3%)
  local copies, waits for them, and re-layouts  2.15 us (2%)
    all_to_all x6, blocking collectives, exchange(): lax.all_to_all(array, axis, 0, 0, axis_index_groups=groups, tiled=True)  104 us
    all_to_all x1, waiting for transfers between devices, exchange(): lax.all_to_all(array, axis, 0, 0, axis_index_groups=groups, tiled=True)  12.1 us
    pallas_call x1, Pallas kernels, grouped_sums(): pl.pallas_call(grouped_kernel, out_shape=jax.ShapeDtypeStruct((16, channe...  6.61 us
    all_to_all x1, starting transfers between devices, exchange(): lax.all_to_all(array, axis, 0, 0, axis_index_groups=groups, tiled=True)  3.83 us
  transfers between devices with their start and end apart: 1, of which 1 were waited for; matrix products, arithmetic and copies ran while one was open for 0% of the time, Pallas kernels for 0%

profile of v2, /device:TPU:1, one launch (start us, length us, event | category | flops | bytes accessed | tf_op | source)
XLA Modules:
  0.0 131.8 jit_solution(388630958962322313)
XLA Ops:
  0.6 0.0 copy-start.5
  0.6 0.0 copy-start.4
  0.7 0.0 copy-start.3
  0.7 0.0 copy-start.2
  0.7 0.0 copy-start.1
  0.7 0.0 copy-start
  0.7 6.6 %grouped_sums.1 = bf16[16,128,128]{2,1,0:T(8,128)(2,1)} custom-call(s32[8]{0:T(128)} %data_tag.1, s32[8]{0:T(128)} %charge_tag.1, s32[8]{0:T(128)} %spin_tag.1, s32[8]{0:T(128)} %atoms_ref.1, s32[8]{0:T(128)} %edges_ref.1, bf16[8,128,256]{2,1,0:T(8,128)(2,1)} %feat_ref.1, bf16[8,128,256]{2,1,0:T(8,128)(2,1)} %cot_ref.1, f32[8,1536]{1,0:T(8,128)} %length_ref.1, ...), custom_call_target="tpu_custom_call" | custom-call | tf_op jit(solution)/shard_map/grouped_sums/pallas_call | solution.py:90
  7.3 21.4 %all_to_all.35 = bf16[16,128,128]{2,1,0:T(8,128)(2,1)S(1)} all-to-all(bf16[16,128,128]{2,1,0:T(8,128)(2,1)} %grouped_sums.1), channel_id=1, replica_groups=mesh['shard'=32,'rep'=16] {'rep'}, dimensions={0} | all-to-all | bytes 1048576 | tf_op jit(solution)/shard_map/all_to_all | solution.py:197
  28.8 0.1 convert_reduce_fusion
  28.8 26.6 %all_to_all.36 = f32[32,4,128]{2,1,0:T(4,128)S(1)} all-to-all(f32[32,4,128]{2,1,0:T(4,128)S(1)} %bitcast.19), channel_id=1, replica_groups=mesh['shard'=32,'rep'=16] {'shard'}, dimensions={0} | all-to-all | bytes 131072 | tf_op jit(solution)/shard_map/all_to_all | solution.py:197
  55.5 13.0 %all_to_all.37 = f32[16,4,128]{2,1,0:T(4,128)S(1)} all-to-all(f32[16,4,128]{2,1,0:T(4,128)S(1)} %broadcast_in_dim.6), channel_id=1, replica_groups=mesh['shard'=32,'rep'=16] {'rep'}, dimensions={0} | all-to-all | bytes 65536 | tf_op jit(solution)/shard_map/all_to_all | solution.py:197
  68.5 0.0 copy-done.5
  68.5 0.0 copy-done.4
  68.5 0.0 copy-done.3
  68.5 1.1 expert_grads.1
  69.6 3.8 %all-to-all-start.3 = ((f32[32,1,128]{2,1,0:T(1,128)}), f32[32,1,128]{2,1,0:T(1,128)S(1)}, u32[]{:S(2)}, u32[]{:S(2)}) async-start(f32[32,1,128]{2,1,0:T(1,128)} %get-tuple-element.10), calls=%async_computation.3 | async-start | bytes 32768 | tf_op jit(solution)/shard_map/all_to_all | solution.py:197
  73.4 12.1 %all-to-all-done.3.square_ref = f32[32,1,128]{2,1,0:T(1,128)S(1)} async-done(((f32[32,1,128]{2,1,0:T(1,128)}), f32[32,1,128]{2,1,0:T(1,128)S(1)}, u32[]{:S(2)}, u32[]{:S(2)}) %all-to-all-start.3) | async-done | bytes 16416 | tf_op jit(solution)/shard_map/all_to_all | solution.py:197
  85.6 0.9 adam_update.1
  86.5 17.8 %all_to_all.38 = bf16[32,16,128]{2,1,0:T(8,128)(2,1)S(1)} all-to-all(bf16[32,16,128]{2,1,0:T(8,128)(2,1)S(1)} %get-tuple-element.15), channel_id=1, replica_groups=mesh['shard'=32,'rep'=16] {'shard'}, dimensions={0} | all-to-all | bytes 262144 | tf_op jit(solution)/shard_map/all_to_all | solution.py:197
  104.4 0.2 broadcast_in_dim.7
  104.6 16.4 %all_to_all.39 = bf16[8,2,32,8,128]{4,3,2,1,0:T(8,128)(2,1)S(1)} all-to-all(bf16[8,2,32,8,128]{4,3,2,1,0:T(8,128)(2,1)S(1)} %broadcast_in_dim.7), channel_id=1, replica_groups={{0,2,4,6,8,10,12,14},{1,3,5,7,9,11,13,15},{16,18,20,22,24,26,28,30},{17..., dimensions={0} | all-to-all | bytes 2097152 | tf_op jit(solution)/shard_map/all_to_all | solution.py:197
  121.0 0.6 broadcast_in_dim.8
  121.6 8.9 %all_to_all.40 = bf16[2,8,2,32,8,128]{5,4,3,2,1,0:T(8,128)(2,1)S(1)} all-to-all(bf16[2,8,2,32,8,128]{5,4,3,2,1,0:T(8,128)(2,1)S(1)} %broadcast_in_dim.8), channel_id=1, replica_groups={{0,1},{2,3},{4,5},{6,7},{8,9},{10,11},{12,13},{14,15},{16,17},{18,19},{..., dimensions={0} | all-to-all | bytes 4194304 | tf_op jit(solution)/shard_map/all_to_all | solution.py:197
  130.5 1.3 %copy.26 = bf16[32,128,2,128]{3,2,1,0:T(2,128)(2,1)} copy(bf16[32,128,2,128]{3,2,1,0:T(2,128)(2,1)S(1)} %bitcast.17) | data formatting | bytes 4194304
  (6 shorter events, 0.1 us)
Async XLA Ops:
  0.6 67.9 %copy-start.5 = (f32[2,32]{1,0:T(2,128)S(1)}, f32[2,32]{1,0:T(2,128)}, u32[]{:S(2)}) copy-start(f32[2,32]{1,0:T(2,128)} %spin_ref.1) | copy-start | bytes 772
  0.6 67.9 %copy-start.4 = (f32[2,32]{1,0:T(2,128)S(1)}, f32[2,32]{1,0:T(2,128)}, u32[]{:S(2)}) copy-start(f32[2,32]{1,0:T(2,128)} %charge_ref.1) | copy-start | bytes 772
  0.7 67.8 %copy-start.3 = (f32[2,32]{1,0:T(2,128)S(1)}, f32[2,32]{1,0:T(2,128)}, u32[]{:S(2)}) copy-start(f32[2,32]{1,0:T(2,128)} %data_ref.1) | copy-start | bytes 772
  0.7 84.9 %copy-start.2 = (f32[32,4,2,128]{3,2,1,0:T(2,128)S(1)}, f32[32,4,2,128]{3,2,1,0:T(2,128)}, u32[]{:S(2)}) copy-start(f32[32,4,2,128]{3,2,1,0:T(2,128)} %param.31) | copy-start | bytes 393220
  0.7 84.9 %copy-start.1 = (f32[32,4,2,128]{3,2,1,0:T(2,128)S(1)}, f32[32,4,2,128]{3,2,1,0:T(2,128)}, u32[]{:S(2)}) copy-start(f32[32,4,2,128]{3,2,1,0:T(2,128)} %param.30) | copy-start | bytes 393220
  0.7 84.9 %copy-start = (f32[32,4,2,128]{3,2,1,0:T(2,128)S(1)}, f32[32,4,2,128]{3,2,1,0:T(2,128)}, u32[]{:S(2)}) copy-start(f32[32,4,2,128]{3,2,1,0:T(2,128)} %param.29) | copy-start | bytes 393220
  69.6 16.0 %all-to-all-start.3 = ((f32[32,1,128]{2,1,0:T(1,128)}), f32[32,1,128]{2,1,0:T(1,128)S(1)}, u32[]{:S(2)}, u32[]{:S(2)}) async-start(f32[32,1,128]{2,1,0:T(1,128)} %get-tuple-element.10), calls=%async_computation.3 | async-start | bytes 32768 | tf_op jit(solution)/shard_map/all_to_all | solution.py:197

commit v3 on v2

--- a/solution.py
+++ b/solution.py
@@ -17,7 +17,6 @@
 decay_rate = 0.01
 cutoff_radius = 6.0
 
-HELD = 4
 PARAMS = pltpu.CompilerParams(vmem_limit_bytes=24 * 2**20)
 
 
@@ -40,69 +39,65 @@
     out_ref,
     total,
 ):
-    step = pl.program_id(0)
-    held, atom_slots, width = feat_ref.shape
+    systems, atom_slots, width = feat_ref.shape
     channels = width // 2
     slots = length_ref.shape[1]
-
-    @pl.when(step == 0)
-    def _():
-        total[...] = jnp.zeros_like(total)
+    total[...] = jnp.zeros_like(total)
 
     atom_ids = lax.broadcasted_iota(jnp.int32, (atom_slots, slots), 0)
     atom_ids = atom_ids.astype(jnp.float32).astype(jnp.bfloat16)
     zero = jnp.zeros((atom_slots, slots), jnp.bfloat16)
     one = jnp.ones((atom_slots, slots), jnp.bfloat16)
-    slot_ids = lax.broadcasted_iota(jnp.int32, (1, slots), 1)
-    for index in range(held):
-        system = step * held + index
-        row = pl.ds(system, 1)
-        atoms_here = jnp.full((1, slots), atoms_ref[system], jnp.int32).astype(jnp.float32)
-        weight = envelope(length_ref[row, :]) * (float(atom_slots) / atoms_here)
-        weight = jnp.where(slot_ids < edges_ref[system], weight, 0.0).astype(jnp.bfloat16)
-        source = source_ref[row, :].astype(jnp.float32).astype(jnp.bfloat16)
-        target = target_ref[row, :].astype(jnp.float32).astype(jnp.bfloat16)
-        links = lax.dot_general(
-            jnp.where(atom_ids == source, weight, zero),
-            jnp.where(atom_ids == target, one, zero),
-            (((1,), (1,)), ((), ())),
+    system_ids = lax.broadcasted_iota(jnp.int32, (systems, slots), 0)
+    slot_ids = lax.broadcasted_iota(jnp.int32, (systems, slots), 1)
+    atoms = jnp.zeros((systems, slots), jnp.int32)
+    edges = jnp.zeros((systems, slots), jnp.int32)
+    for system in range(systems):
+        atoms = jnp.where(system_ids == system, atoms_ref[system], atoms)
+        edges = jnp.where(system_ids == system, edges_ref[system], edges)
+    weight = envelope(length_ref[...]) * (float(atom_slots) / atoms.astype(jnp.float32))
+    weight = jnp.where(slot_ids < edges, weight, 0.0).astype(jnp.bfloat16)
+    source = source_ref[...].astype(jnp.float32).astype(jnp.bfloat16)
+    target = target_ref[...].astype(jnp.float32).astype(jnp.bfloat16)
+
+    links = []
+    for system in range(systems):
+        row = slice(system, system + 1)
+        links.append(
+            lax.dot_general(
+                jnp.where(atom_ids == source[row], weight[row], zero),
+                jnp.where(atom_ids == target[row], one, zero),
+                (((1,), (1,)), ((), ())),
+                preferred_element_type=jnp.float32,
+            ).astype(jnp.bfloat16)
+        )
+    for system in range(systems):
+        mixed = jnp.dot(links[system], cot_ref[system], preferred_element_type=jnp.float32)
+        mixed = mixed.astype(jnp.bfloat16)
+        swapped = jnp.concatenate([mixed[:, channels:], -mixed[:, :channels]], axis=1)
+        feat = feat_ref[system]
+        product = jnp.dot(
+            jnp.concatenate([feat[:, :channels].T, feat[:, channels:].T], axis=1),
+            jnp.concatenate([mixed, swapped], axis=0),
             preferred_element_type=jnp.float32,
-        ).astype(jnp.bfloat16)
-        mixed = jnp.dot(links, cot_ref[index], preferred_element_type=jnp.float32)
-        product = jnp.dot(
-            feat_ref[index].T, mixed.astype(jnp.bfloat16), preferred_element_type=jnp.float32
         )
         tag = (data_tag[system] * 2 + charge_tag[system]) * 2 + spin_tag[system]
-        total[2 * tag] += product[:channels, :channels] + product[channels:, channels:]
-        total[2 * tag + 1] += product[:channels, channels:] - product[channels:, :channels]
-
-    @pl.when(step == pl.num_programs(0) - 1)
-    def _():
-        out_ref[...] = total[...].astype(out_ref.dtype)
+        total[2 * tag] += product[:, :channels]
+        total[2 * tag + 1] += product[:, channels:]
+    out_ref[...] = total[...].astype(out_ref.dtype)
 
 
 def grouped_sums(feat, cot, length, atoms, edges, source, target, data_tag, charge_tag, spin_tag):
-    systems, atom_slots, width = feat.shape
-    channels = width // 2
-    slots = length.shape[1]
-    whole = lambda i, *_: (0, 0)
-    each = lambda i, *_: (i, 0, 0)
+    channels = feat.shape[2] // 2
+    block = lambda shape: pl.BlockSpec(shape, lambda i: (0,) * len(shape))
     return pl.pallas_call(
         grouped_kernel,
         out_shape=jax.ShapeDtypeStruct((16, channels, channels), jnp.bfloat16),
-        grid_spec=pltpu.PrefetchScalarGridSpec(
-            num_scalar_prefetch=5,
-            grid=(systems // HELD,),
-            in_specs=[
-                pl.BlockSpec((HELD, atom_slots, width), each),
-                pl.BlockSpec((HELD, atom_slots, width), each),
-                pl.BlockSpec((systems, slots), whole),
-                pl.BlockSpec((systems, slots), whole),
-                pl.BlockSpec((systems, slots), whole),
-            ],
-            out_specs=pl.BlockSpec((16, channels, channels), lambda i, *_: (0, 0, 0)),
-            scratch_shapes=[pltpu.VMEM((16, channels, channels), jnp.float32)],
-        ),
+        grid=(1,),
+        in_specs=[pl.BlockSpec(memory_space=pltpu.SMEM)] * 5
+        + [block(array.shape) for array in (feat, cot, length, source, target)],
+        out_specs=block((16, channels, channels)),
+        scratch_shapes=[pltpu.VMEM((16, channels, channels), jnp.float32)],
         name="grouped_sums",
     )(data_tag, charge_tag, spin_tag, atoms, edges, feat, cot, length, source, target)
 
@@ -193,6 +188,35 @@
     )(first, squares, grads, params, moment_one, moment_two)
 
 
+def place_kernel(offset, core_ref, *refs):
+    half_ref, out_ref, sem = refs[0], refs[-2], refs[-1]
+    side = jnp.bitwise_xor(core_ref[0], offset)
+    copy = pltpu.make_async_copy(half_ref, out_ref.at[side], sem)
+    copy.start()
+    copy.wait()
+
+
+def place_half(offset, core, half, *held):
+    hbm = pl.BlockSpec(memory_space=pl.ANY)
+    return pl.pallas_call(
+        functools.partial(place_kernel, offset),
+        out_shape=jax.ShapeDtypeStruct((2,) + half.shape, half.dtype),
+        in_specs=[
+            pl.BlockSpec(memory_space=pltpu.SMEM),
+            pl.BlockSpec(memory_space=pltpu.VMEM),
+        ]
+        + [hbm] * len(held),
+        out_specs=hbm,
+        scratch_shapes=[pltpu.SemaphoreType.DMA],
+        input_output_aliases={2: 0} if held else {},
+        compiler_params=PARAMS,
+        cost_estimate=pl.CostEstimate(
+            flops=0, transcendentals=0, bytes_accessed=2 * half.size * half.dtype.itemsize
+        ),
+        name="place_half",
+    )(core, half, *held)
+
+
 def exchange(array, axis, groups=None):
     return lax.all_to_all(array, axis, 0, 0, axis_index_groups=groups, tiled=True)
 
@@ -257,9 +281,10 @@
     share = exchange(share, "shard").reshape(shards, 2, own * 2, channels)
     share = jnp.broadcast_to(jnp.swapaxes(share, 0, 1)[None], (8, 2, shards, own * 2, channels))
     share = exchange(share, "rep", [[2 * i + core for i in range(8)] for core in range(2)])
-    share = jnp.broadcast_to(share[None], (2,) + share.shape)
-    share = exchange(share, "rep", [[2 * i, 2 * i + 1] for i in range(8)])
-    full_weights = share.reshape(experts, shards * own, 2, channels)
+    core = jnp.bitwise_and(place, 1).reshape(1)
+    other = lax.ppermute(share, "rep", [(i, i ^ 1) for i in range(reps)])
+    full_weights = place_half(1, core, other, place_half(0, core, share))
+    full_weights = full_weights.reshape(experts, shards * own, 2, channels)
     return (new_params.reshape(shape), new_one.reshape(shape), new_two.reshape(shape), full_weights)
 
 

time: 132 us -> 127 us (0.962)
  blocking collectives: 104 us -> 95.3 us
  starting transfers between devices: 3.83 us -> 9.57 us
  local copies, waits for them, and re-layouts: 2.15 us -> 0.24 us
    all_to_all x6 -> x5, blocking collectives: 104 us -> 95.3 us  [exchange(): lax.all_to_all(array, axis, 0, 0, axis_index_groups=groups, tiled=True)]
    ppermute x0 -> x1, starting transfers between devices: none -> 5.74 us  [local(): other = lax.ppermute(share, 'rep', [(i, i ^ 1) for i in range(reps)])]
    pallas_call x1, Pallas kernels: 6.61 us -> 3.63 us  [grouped_sums(): pl.pallas_call(grouped_kernel, out_shape=jax.ShapeDtypeStruct((16, channe...]
    pallas_call x0 -> x2, Pallas kernels: none -> 1.96 us  [place_half(): pl.pallas_call(functools.partial(place_kernel, offset), out_shape=jax.Sha...]
  transfers between devices with their start and end apart: 1 -> 2, of which waited for: 1 -> 2; matrix products, arithmetic and copies ran while one was open for 0% -> 0% of each run, Pallas kernels for 0% -> 1%
where the time goes in v3:
time: 127 us
  blocking collectives  95.3 us (75%)
  waiting for transfers between devices  13.4 us (11%)
  starting transfers between devices  9.57 us (8%)
  Pallas kernels  7.6 us (6%)
    all_to_all x5, blocking collectives, exchange(): lax.all_to_all(array, axis, 0, 0, axis_index_groups=groups, tiled=True)  95.3 us
    all_to_all x1, waiting for transfers between devices, exchange(): lax.all_to_all(array, axis, 0, 0, axis_index_groups=groups, tiled=True)  12.1 us
    ppermute x1, starting transfers between devices, local(): other = lax.ppermute(share, 'rep', [(i, i ^ 1) for i in range(reps)])  5.74 us
    all_to_all x1, starting transfers between devices, exchange(): lax.all_to_all(array, axis, 0, 0, axis_index_groups=groups, tiled=True)  3.83 us
    pallas_call x1, Pallas kernels, grouped_sums(): pl.pallas_call(grouped_kernel, out_shape=jax.ShapeDtypeStruct((16, channe...  3.63 us
  transfers between devices with their start and end apart: 2, of which 2 were waited for; matrix products, arithmetic and copies ran while one was open for 0% of the time, Pallas kernels for 1%

profile of v3, /device:TPU:1, one launch (start us, length us, event | category | flops | bytes accessed | tf_op | source)
XLA Modules:
  0.0 127.0 jit_solution(1422075781489142098)
XLA Ops:
  0.6 0.0 copy-start.5
  0.6 0.0 copy-start.4
  0.7 0.0 copy-start.3
  0.7 0.0 copy-start.2
  0.7 0.0 copy-start.1
  0.7 0.0 copy-start
  0.7 3.6 %grouped_sums.1 = bf16[16,128,128]{2,1,0:T(8,128)(2,1)} custom-call(s32[8]{0:T(128)} %data_tag.1, s32[8]{0:T(128)} %charge_tag.1, s32[8]{0:T(128)} %spin_tag.1, s32[8]{0:T(128)} %atoms_ref.1, s32[8]{0:T(128)} %edges_ref.1, bf16[8,128,256]{2,1,0:T(8,128)(2,1)} %feat_ref.1, bf16[8,128,256]{2,1,0:T(8,128)(2,1)} %cot_ref.1, f32[8,1536]{1,0:T(8,128)} %length_ref.1, ...), custom_call_target="tpu_custom_call" | custom-call | tf_op jit(solution)/shard_map/grouped_sums/pallas_call | solution.py:93
  4.3 21.4 %all_to_all.30 = bf16[16,128,128]{2,1,0:T(8,128)(2,1)S(1)} all-to-all(bf16[16,128,128]{2,1,0:T(8,128)(2,1)} %grouped_sums.1), channel_id=1, replica_groups=mesh['shard'=32,'rep'=16] {'rep'}, dimensions={0} | all-to-all | bytes 1048576 | tf_op jit(solution)/shard_map/all_to_all | solution.py:221
  25.8 0.1 convert_reduce_fusion
  25.8 26.6 %all_to_all.31 = f32[32,4,128]{2,1,0:T(4,128)S(1)} all-to-all(f32[32,4,128]{2,1,0:T(4,128)S(1)} %bitcast.21), channel_id=1, replica_groups=mesh['shard'=32,'rep'=16] {'shard'}, dimensions={0} | all-to-all | bytes 131072 | tf_op jit(solution)/shard_map/all_to_all | solution.py:221
  52.5 13.0 %all_to_all.32 = f32[16,4,128]{2,1,0:T(4,128)S(1)} all-to-all(f32[16,4,128]{2,1,0:T(4,128)S(1)} %broadcast_in_dim.4), channel_id=1, replica_groups=mesh['shard'=32,'rep'=16] {'rep'}, dimensions={0} | all-to-all | bytes 65536 | tf_op jit(solution)/shard_map/all_to_all | solution.py:221
  65.5 1.1 expert_grads.1
  66.6 3.8 %all-to-all-start.3 = ((f32[32,1,128]{2,1,0:T(1,128)}), f32[32,1,128]{2,1,0:T(1,128)S(1)}, u32[]{:S(2)}, u32[]{:S(2)}) async-start(f32[32,1,128]{2,1,0:T(1,128)} %get-tuple-element.10), calls=%async_computation.3 | async-start | bytes 32768 | tf_op jit(solution)/shard_map/all_to_all | solution.py:221
  70.4 12.1 %all-to-all-done.3.square_ref = f32[32,1,128]{2,1,0:T(1,128)S(1)} async-done(((f32[32,1,128]{2,1,0:T(1,128)}), f32[32,1,128]{2,1,0:T(1,128)S(1)}, u32[]{:S(2)}, u32[]{:S(2)}) %all-to-all-start.3) | async-done | bytes 16416 | tf_op jit(solution)/shard_map/all_to_all | solution.py:221
  82.6 0.0 copy-done.2
  82.6 0.0 copy-done
  82.6 0.9 adam_update.1
  83.5 17.8 %all_to_all.33 = bf16[32,16,128]{2,1,0:T(8,128)(2,1)S(1)} all-to-all(bf16[32,16,128]{2,1,0:T(8,128)(2,1)S(1)} %get-tuple-element.15), channel_id=1, replica_groups=mesh['shard'=32,'rep'=16] {'shard'}, dimensions={0} | all-to-all | bytes 262144 | tf_op jit(solution)/shard_map/all_to_all | solution.py:221
  101.4 0.2 broadcast_in_dim.5
  101.6 16.4 %all_to_all.34.refs_0_ = bf16[8,2,32,8,128]{4,3,2,1,0:T(8,128)(2,1)S(1)} all-to-all(bf16[8,2,32,8,128]{4,3,2,1,0:T(8,128)(2,1)S(1)} %broadcast_in_dim.5), channel_id=1, replica_groups={{0,2,4,6,8,10,12,14},{1,3,5,7,9,11,13,15},{16,18,20,22,24,26,28,30},{17..., dimensions={0} | all-to-all | bytes 2097152 | tf_op jit(solution)/shard_map/all_to_all | solution.py:221
  118.0 5.7 %collective-permute-start = (bf16[8,2,32,8,128]{4,3,2,1,0:T(8,128)(2,1)S(1)}, bf16[8,2,32,8,128]{4,3,2,1,0:T(8,128)(2,1)S(1)}, u32[]{:S(2)}, u32[]{:S(2)}) collective-permute-start(bf16[8,2,32,8,128]{4,3,2,1,0:T(8,128)(2,1)S(1)} %all_to_all.34.refs_0_), channel_id=1, source_target_pairs={{0,1},{1,0},{2,3},{3,2},{4,5},{5,4},{6,7},{7,6},{8,9},{9,8},{10,11... | collective-permute-start | bytes 3145736 | tf_op jit(solution)/shard_map/ppermute | solution.py:285
  123.7 1.0 place_half.2.refs_1_
  124.7 1.3 %collective-permute-done.refs_0_ = bf16[8,2,32,8,128]{4,3,2,1,0:T(8,128)(2,1)S(1)} collective-permute-done((bf16[8,2,32,8,128]{4,3,2,1,0:T(8,128)(2,1)S(1)}, bf16[8,2,32,8,128]{4,3,2,1,0:T(8,128)(2,1)S(1)}, u32[]{:S(2)}, u32[]{:S(2)}) %collective-permute-start) | collective-permute-done | bytes 1048608 | tf_op jit(solution)/shard_map/ppermute | solution.py:285
  126.0 1.0 place_half.3
  (7 shorter events, 0.1 us)
Async XLA Ops:
  0.6 64.9 %copy-start.5 = (f32[2,32]{1,0:T(2,128)S(1)}, f32[2,32]{1,0:T(2,128)}, u32[]{:S(2)}) copy-start(f32[2,32]{1,0:T(2,128)} %spin_ref.1) | copy-start | bytes 772
  0.6 64.9 %copy-start.4 = (f32[2,32]{1,0:T(2,128)S(1)}, f32[2,32]{1,0:T(2,128)}, u32[]{:S(2)}) copy-start(f32[2,32]{1,0:T(2,128)} %charge_ref.1) | copy-start | bytes 772
  0.7 64.9 %copy-start.3 = (f32[2,32]{1,0:T(2,128)S(1)}, f32[2,32]{1,0:T(2,128)}, u32[]{:S(2)}) copy-start(f32[2,32]{1,0:T(2,128)} %data_ref.1) | copy-start | bytes 772
  0.7 81.9 %copy-start.2 = (f32[32,4,2,128]{3,2,1,0:T(2,128)S(1)}, f32[32,4,2,128]{3,2,1,0:T(2,128)}, u32[]{:S(2)}) copy-start(f32[32,4,2,128]{3,2,1,0:T(2,128)} %param.31) | copy-start | bytes 393220
  0.7 81.9 %copy-start.1 = (f32[32,4,2,128]{3,2,1,0:T(2,128)S(1)}, f32[32,4,2,128]{3,2,1,0:T(2,128)}, u32[]{:S(2)}) copy-start(f32[32,4,2,128]{3,2,1,0:T(2,128)} %param.30) | copy-start | bytes 393220
  0.7 81.9 %copy-start = (f32[32,4,2,128]{3,2,1,0:T(2,128)S(1)}, f32[32,4,2,128]{3,2,1,0:T(2,128)}, u32[]{:S(2)}) copy-start(f32[32,4,2,128]{3,2,1,0:T(2,128)} %param.29) | copy-start | bytes 393220
  66.6 16.0 %all-to-all-start.3 = ((f32[32,1,128]{2,1,0:T(1,128)}), f32[32,1,128]{2,1,0:T(1,128)S(1)}, u32[]{:S(2)}, u32[]{:S(2)}) async-start(f32[32,1,128]{2,1,0:T(1,128)} %get-tuple-element.10), calls=%async_computation.3 | async-start | bytes 32768 | tf_op jit(solution)/shard_map/all_to_all | solution.py:221
  118.0 8.0 %collective-permute-start = (bf16[8,2,32,8,128]{4,3,2,1,0:T(8,128)(2,1)S(1)}, bf16[8,2,32,8,128]{4,3,2,1,0:T(8,128)(2,1)S(1)}, u32[]{:S(2)}, u32[]{:S(2)}) collective-permute-start(bf16[8,2,32,8,128]{4,3,2,1,0:T(8,128)(2,1)S(1)} %all_to_all.34.refs_0_), channel_id=1, source_target_pairs={{0,1},{1,0},{2,3},{3,2},{4,5},{5,4},{6,7},{7,6},{8,9},{9,8},{10,11... | collective-permute-start | bytes 3145736 | tf_op jit(solution)/shard_map/ppermute | solution.py:285

commit v4 on v3

--- a/solution.py
+++ b/solution.py
@@ -84,7 +84,10 @@
         tag = (data_tag[system] * 2 + charge_tag[system]) * 2 + spin_tag[system]
         total[2 * tag] += product[:, :channels]
         total[2 * tag + 1] += product[:, channels:]
-    out_ref[...] = total[...].astype(out_ref.dtype)
+    half = channels // 2
+    for side in range(2):
+        rows = pl.ds(side * half, half)
+        out_ref[pl.ds(16 * side, 16)] = total[:, rows, :].astype(out_ref.dtype)
 
 
 def grouped_sums(feat, cot, length, atoms, edges, source, target, data_tag, charge_tag, spin_tag):
@@ -92,11 +95,11 @@
     block = lambda shape: pl.BlockSpec(shape, lambda i: (0,) * len(shape))
     return pl.pallas_call(
         grouped_kernel,
-        out_shape=jax.ShapeDtypeStruct((16, channels, channels), jnp.bfloat16),
+        out_shape=jax.ShapeDtypeStruct((32, channels // 2, channels), jnp.bfloat16),
         grid=(1,),
         in_specs=[pl.BlockSpec(memory_space=pltpu.SMEM)] * 5
         + [block(array.shape) for array in (feat, cot, length, source, target)],
-        out_specs=block((16, channels, channels)),
+        out_specs=block((32, channels // 2, channels)),
         scratch_shapes=[pltpu.VMEM((16, channels, channels), jnp.float32)],
         name="grouped_sums",
     )(data_tag, charge_tag, spin_tag, atoms, edges, feat, cot, length, source, target)
@@ -175,12 +178,11 @@
 
 
 def adam_update(first, squares, grads, params, moment_one, moment_two, norm_limit):
-    shards = squares.shape[0]
     state = jax.ShapeDtypeStruct(params.shape, jnp.float32)
     vmem = pl.BlockSpec(memory_space=pltpu.VMEM)
     return pl.pallas_call(
         functools.partial(adam_kernel, norm_limit),
-        out_shape=(state, state, state, jax.ShapeDtypeStruct((shards, 16, 128), jnp.bfloat16)),
+        out_shape=(state, state, state, jax.ShapeDtypeStruct((16, 16, 128), jnp.bfloat16)),
         in_specs=[pl.BlockSpec(memory_space=pltpu.SMEM)] + [vmem] * 5,
         out_specs=(vmem,) * 4,
         compiler_params=PARAMS,
@@ -189,25 +191,33 @@
 
 
 def place_kernel(offset, core_ref, *refs):
-    half_ref, out_ref, sem = refs[0], refs[-2], refs[-1]
+    half_ref, out_ref, sems = refs[0], refs[-2], refs[-1]
     side = jnp.bitwise_xor(core_ref[0], offset)
-    copy = pltpu.make_async_copy(half_ref, out_ref.at[side], sem)
-    copy.start()
-    copy.wait()
+    copies = [
+        pltpu.make_async_copy(
+            half_ref.at[:, low, expert], out_ref.at[side, :, expert, low], sems.at[2 * low + expert]
+        )
+        for low in range(2)
+        for expert in range(2)
+    ]
+    for copy in copies:
+        copy.start()
+    for copy in copies:
+        copy.wait()
 
 
 def place_half(offset, core, half, *held):
     hbm = pl.BlockSpec(memory_space=pl.ANY)
     return pl.pallas_call(
         functools.partial(place_kernel, offset),
-        out_shape=jax.ShapeDtypeStruct((2,) + half.shape, half.dtype),
+        out_shape=jax.ShapeDtypeStruct((2, 8, 2, 2) + half.shape[3:], half.dtype),
         in_specs=[
             pl.BlockSpec(memory_space=pltpu.SMEM),
             pl.BlockSpec(memory_space=pltpu.VMEM),
         ]
         + [hbm] * len(held),
         out_specs=hbm,
-        scratch_shapes=[pltpu.SemaphoreType.DMA],
+        scratch_shapes=[pltpu.SemaphoreType.DMA((4,))],
         input_output_aliases={2: 0} if held else {},
         compiler_params=PARAMS,
         cost_estimate=pl.CostEstimate(
@@ -246,6 +256,10 @@
     rows = (experts, own * 2, channels)
     place = lax.axis_index("rep")
     first = jnp.bitwise_and(place, 1) * (experts // 2) + jnp.bitwise_and(place, reps - 2)
+    core = jnp.bitwise_and(place, 1)
+    dataset_tag, first, core = lax.optimization_barrier(
+        (dataset_tag, first.reshape(1), core.reshape(1))
+    )
 
     sums = grouped_sums(
         node_feat,
@@ -259,9 +273,17 @@
         charge_tag,
         spin_tag,
     )
-    sums = exchange(sums, "rep")
-    sums = jnp.sum(sums.astype(jnp.float32), axis=0).reshape(shards, own, channels)
-    sums = exchange(sums, "shard")
+    both = ("shard", "rep")
+    planes = [[(16 * low + z) * reps + i for low in range(2) for i in range(reps)] for z in range(16)]
+    columns = [[16 * low + z for z in range(16)] for low in range(2)]
+    cores = [
+        [(16 * low + z) * reps + 2 * i + core for i in range(8) for low in range(2)]
+        for z in range(16)
+        for core in range(2)
+    ]
+    sums = exchange(sums, both, planes)
+    sums = jnp.sum(sums.astype(jnp.float32), axis=0).reshape(16, own, channels)
+    sums = exchange(sums, "shard", columns)
     sums = jnp.sum(sums, axis=0)
     sums = exchange(jnp.broadcast_to(sums[None], (reps, own, channels)), "rep")
     grads, squares = expert_grads(
@@ -270,7 +292,7 @@
     squares = exchange(squares, "shard")
     norm_limit = math.sqrt(experts * 2 * channels * channels)
     new_params, new_one, new_two, share = adam_update(
-        first.reshape(1),
+        first,
         squares,
         grads,
         params.reshape(rows),
@@ -278,10 +300,9 @@
         moment_two.reshape(rows),
         norm_limit,
     )
-    share = exchange(share, "shard").reshape(shards, 2, own * 2, channels)
-    share = jnp.broadcast_to(jnp.swapaxes(share, 0, 1)[None], (8, 2, shards, own * 2, channels))
-    share = exchange(share, "rep", [[2 * i + core for i in range(8)] for core in range(2)])
-    core = jnp.bitwise_and(place, 1).reshape(1)
+    share = exchange(share, "shard", columns).reshape(16, 2, own * 2, channels)
+    share = jnp.broadcast_to(jnp.swapaxes(share, 0, 1)[None], (16, 2, 16, own * 2, channels))
+    share = exchange(share, both, cores).reshape(8, 2, 2, 16, own * 2, channels)
     other = lax.ppermute(share, "rep", [(i, i ^ 1) for i in range(reps)])
     full_weights = place_half(1, core, other, place_half(0, core, share))
     full_weights = full_weights.reshape(experts, shards * own, 2, channels)

time: 127 us -> 120 us (0.945)
  waiting for transfers between devices: 13.4 us -> 1.26 us
  blocking collectives: 95.3 us -> 105 us
  starting transfers between devices: 9.57 us -> 5.51 us
    all_to_all x1 -> x0, waiting for transfers between devices: 12.1 us -> none  [exchange(): lax.all_to_all(array, axis, 0, 0, axis_index_groups=groups, tiled=True)]
    all_to_all x5 -> x6, blocking collectives: 95.3 us -> 105 us  [exchange(): lax.all_to_all(array, axis, 0, 0, axis_index_groups=groups, tiled=True)]
    all_to_all x1 -> x0, starting transfers between devices: 3.83 us -> none  [exchange(): lax.all_to_all(array, axis, 0, 0, axis_index_groups=groups, tiled=True)]
  transfers between devices with their start and end apart: 2 -> 1, of which waited for: 2 -> 1; matrix products, arithmetic and copies ran while one was open for 0% -> 0% of each run, Pallas kernels for 1% -> 1%
where the time goes in v4:
time: 120 us
  blocking collectives  105 us (88%)
  Pallas kernels  7.04 us (6%)
  starting transfers between devices  5.51 us (5%)
  waiting for transfers between devices  1.26 us (1%)
    all_to_all x6, blocking collectives, exchange(): lax.all_to_all(array, axis, 0, 0, axis_index_groups=groups, tiled=True)  105 us
    ppermute x1, starting transfers between devices, local(): other = lax.ppermute(share, 'rep', [(i, i ^ 1) for i in range(reps)])  5.51 us
    pallas_call x1, Pallas kernels, grouped_sums(): pl.pallas_call(grouped_kernel, out_shape=jax.ShapeDtypeStruct((32, channe...  3.64 us
  transfers between devices with their start and end apart: 1, of which 1 were waited for; matrix products, arithmetic and copies ran while one was open for 0% of the time, Pallas kernels for 1%

profile of v4, /device:TPU:1, one launch (start us, length us, event | category | flops | bytes accessed | tf_op | source)
XLA Modules:
  0.0 120.0 jit_solution(7687718052349226502)
XLA Ops:
  0.6 0.0 copy-start.5
  0.6 0.0 copy-start.4
  0.7 0.0 copy-start.3
  0.7 0.0 copy-start.2
  0.7 0.0 copy-start.1
  0.7 0.0 copy-start
  0.7 3.6 %grouped_sums.1 = bf16[32,64,128]{2,1,0:T(8,128)(2,1)} custom-call(s32[8]{0:T(128)} %data_tag, s32[8]{0:T(128)} %charge_tag.1, s32[8]{0:T(128)} %spin_tag.1, s32[8]{0:T(128)} %atoms_ref.1, s32[8]{0:T(128)} %edges_ref.1, bf16[8,128,256]{2,1,0:T(8,128)(2,1)} %feat_ref.1, bf16[8,128,256]{2,1,0:T(8,128)(2,1)} %cot_ref.1, f32[8,1536]{1,0:T(8,128)} %length_ref.1, ...), custom_call_target="tpu_custom_call" | custom-call | tf_op jit(solution)/shard_map/grouped_sums/pallas_call | solution.py:96
  4.3 21.9 %all_to_all.30 = bf16[32,64,128]{2,1,0:T(8,128)(2,1)S(1)} all-to-all(bf16[32,64,128]{2,1,0:T(8,128)(2,1)} %grouped_sums.1), channel_id=1, replica_groups={{0,1,2,3,4,5,6,7,8,9,10,11,12,13,14,15,256,257,258,259,260,261,262,263,..., dimensions={0} | all-to-all | bytes 1048576 | tf_op jit(solution)/shard_map/all_to_all | solution.py:231
  26.3 0.1 convert_reduce_fusion
  26.4 24.3 %all_to_all.31 = f32[16,4,128]{2,1,0:T(4,128)S(1)} all-to-all(f32[16,4,128]{2,1,0:T(4,128)S(1)} %bitcast.23), channel_id=1, replica_groups={{0,16,32,48,64,80,96,112,128,144,160,176,192,208,224,240},{256,272,288,..., dimensions={0} | all-to-all | bytes 65536 | tf_op jit(solution)/shard_map/all_to_all | solution.py:231
  50.7 12.2 %all_to_all.32 = f32[16,4,128]{2,1,0:T(4,128)S(1)} all-to-all(f32[16,4,128]{2,1,0:T(4,128)S(1)} %broadcast_in_dim.4), channel_id=1, replica_groups=mesh['shard'=32,'rep'=16] {'rep'}, dimensions={0} | all-to-all | bytes 65536 | tf_op jit(solution)/shard_map/all_to_all | solution.py:231
  62.9 0.0 copy-done.5
  62.9 0.0 copy-done.4
  63.0 0.5 expert_grads.1
  63.4 15.2 %all_to_all.33.square_ref = f32[32,1,128]{2,1,0:T(1,128)S(1)} all-to-all(f32[32,1,128]{2,1,0:T(1,128)S(1)} %get-tuple-element.15), channel_id=1, replica_groups=mesh['shard'=32,'rep'=16] {'shard'}, dimensions={0} | all-to-all | bytes 32768 | tf_op jit(solution)/shard_map/all_to_all | solution.py:231
  78.6 0.0 copy-done.1
  78.6 0.9 adam_update.1
  79.6 14.3 %all_to_all.34 = bf16[16,16,128]{2,1,0:T(8,128)(2,1)S(1)} all-to-all(bf16[16,16,128]{2,1,0:T(8,128)(2,1)S(1)} %get-tuple-element.21), channel_id=1, replica_groups={{0,16,32,48,64,80,96,112,128,144,160,176,192,208,224,240},{256,272,288,..., dimensions={0} | all-to-all | bytes 131072 | tf_op jit(solution)/shard_map/all_to_all | solution.py:231
  93.9 0.2 broadcast_in_dim.5
  94.1 17.1 %all_to_all.35 = bf16[16,2,16,8,128]{4,3,2,1,0:T(8,128)(2,1)S(1)} all-to-all(bf16[16,2,16,8,128]{4,3,2,1,0:T(8,128)(2,1)S(1)} %broadcast_in_dim.5), channel_id=1, replica_groups={{0,256,2,258,4,260,6,262,8,264,10,266,12,268,14,270},{1,257,3,259,5,261..., dimensions={0} | all-to-all | bytes 2097152 | tf_op jit(solution)/shard_map/all_to_all | solution.py:231
  111.2 5.5 %collective-permute-start = (bf16[8,2,2,16,8,128]{5,4,3,2,1,0:T(8,128)(2,1)S(1)}, bf16[8,2,2,16,8,128]{5,4,3,2,1,0:T(8,128)(2,1)S(1)}, u32[]{:S(2)}, u32[]{:S(2)}) collective-permute-start(bf16[8,2,2,16,8,128]{5,4,3,2,1,0:T(8,128)(2,1)S(1)} %bitcast.15), channel_id=1, source_target_pairs={{0,1},{1,0},{2,3},{3,2},{4,5},{5,4},{6,7},{7,6},{8,9},{9,8},{10,11... | collective-permute-start | bytes 3145736 | tf_op jit(solution)/shard_map/ppermute | solution.py:306
  116.7 1.0 place_half.2.refs_1_
  117.7 1.3 %collective-permute-done.refs_0_ = bf16[8,2,2,16,8,128]{5,4,3,2,1,0:T(8,128)(2,1)S(1)} collective-permute-done((bf16[8,2,2,16,8,128]{5,4,3,2,1,0:T(8,128)(2,1)S(1)}, bf16[8,2,2,16,8,128]{5,4,3,2,1,0:T(8,128)(2,1)S(1)}, u32[]{:S(2)}, u32[]{:S(2)}) %collective-permute-start) | collective-permute-done | bytes 1048608 | tf_op jit(solution)/shard_map/ppermute | solution.py:306
  119.0 1.0 place_half.3
  (6 shorter events, 0.0 us)
Async XLA Ops:
  0.6 62.3 %copy-start.5 = (f32[2,32]{1,0:T(2,128)S(1)}, f32[2,32]{1,0:T(2,128)}, u32[]{:S(2)}) copy-start(f32[2,32]{1,0:T(2,128)} %spin_ref.1) | copy-start | bytes 772
  0.6 62.3 %copy-start.4 = (f32[2,32]{1,0:T(2,128)S(1)}, f32[2,32]{1,0:T(2,128)}, u32[]{:S(2)}) copy-start(f32[2,32]{1,0:T(2,128)} %charge_ref.1) | copy-start | bytes 772
  0.7 62.3 %copy-start.3 = (f32[2,32]{1,0:T(2,128)S(1)}, f32[2,32]{1,0:T(2,128)}, u32[]{:S(2)}) copy-start(f32[2,32]{1,0:T(2,128)} %data_ref.1) | copy-start | bytes 772
  0.7 77.9 %copy-start.2 = (f32[32,4,2,128]{3,2,1,0:T(2,128)S(1)}, f32[32,4,2,128]{3,2,1,0:T(2,128)}, u32[]{:S(2)}) copy-start(f32[32,4,2,128]{3,2,1,0:T(2,128)} %param.31) | copy-start | bytes 393220
  0.7 77.9 %copy-start.1 = (f32[32,4,2,128]{3,2,1,0:T(2,128)S(1)}, f32[32,4,2,128]{3,2,1,0:T(2,128)}, u32[]{:S(2)}) copy-start(f32[32,4,2,128]{3,2,1,0:T(2,128)} %param.30) | copy-start | bytes 393220
  0.7 77.9 %copy-start = (f32[32,4,2,128]{3,2,1,0:T(2,128)S(1)}, f32[32,4,2,128]{3,2,1,0:T(2,128)}, u32[]{:S(2)}) copy-start(f32[32,4,2,128]{3,2,1,0:T(2,128)} %param.29) | copy-start | bytes 393220
  111.2 7.8 %collective-permute-start = (bf16[8,2,2,16,8,128]{5,4,3,2,1,0:T(8,128)(2,1)S(1)}, bf16[8,2,2,16,8,128]{5,4,3,2,1,0:T(8,128)(2,1)S(1)}, u32[]{:S(2)}, u32[]{:S(2)}) collective-permute-start(bf16[8,2,2,16,8,128]{5,4,3,2,1,0:T(8,128)(2,1)S(1)} %bitcast.15), channel_id=1, source_target_pairs={{0,1},{1,0},{2,3},{3,2},{4,5},{5,4},{6,7},{7,6},{8,9},{9,8},{10,11... | collective-permute-start | bytes 3145736 | tf_op jit(solution)/shard_map/ppermute | solution.py:306

commit v5 on v4

--- a/solution.py
+++ b/solution.py
@@ -105,7 +105,20 @@
     )(data_tag, charge_tag, spin_tag, atoms, edges, feat, cot, length, source, target)
 
 
-def expert_kernel(data_ref, charge_ref, spin_ref, sums_ref, grad_ref, square_ref):
+def expert_kernel(
+    first_ref,
+    low_ref,
+    data_ref,
+    charge_ref,
+    spin_ref,
+    sums_ref,
+    params_ref,
+    one_ref,
+    two_ref,
+    grad_ref,
+    share_ref,
+    held,
+):
     data_gain, charge_gain, spin_gain = data_ref[...], charge_ref[...], spin_ref[...]
     table = jnp.concatenate(
         [
@@ -118,76 +131,125 @@
     )
     mixing = table / jnp.sum(table, axis=1, keepdims=True)
     squares = None
-    for channel in range(4):
-        for part in range(2):
-            rows = sums_ref[:, part, channel, :]
-            grad = lax.dot_general(
-                mixing,
-                rows,
-                (((0,), (0,)), ((), ())),
-                precision=lax.Precision.HIGHEST,
-                preferred_element_type=jnp.float32,
-            )
-            grad_ref[:, 2 * channel + part, :] = grad
-            term = jnp.sum(grad * grad, axis=0, keepdims=True)
-            squares = term if squares is None else squares + term
-    square_ref[...] = jnp.broadcast_to(squares[None], square_ref.shape)
-
-
-def expert_grads(data_gain, charge_gain, spin_gain, sums, shards):
-    experts = data_gain.shape[1]
+    for low in range(2):
+        for channel in range(4):
+            for part in range(2):
+                grad = lax.dot_general(
+                    mixing,
+                    sums_ref[low, :, part, channel, :],
+                    (((0,), (0,)), ((), ())),
+                    precision=lax.Precision.HIGHEST,
+                    preferred_element_type=jnp.float32,
+                )
+                held[low, :, 2 * channel + part, :] = grad
+                term = jnp.sum(grad * grad, axis=0, keepdims=True)
+                squares = term if squares is None else squares + term
+    grad_ref[...] = held[low_ref[0]]
+
+    def rounded(value):
+        return value.astype(jnp.bfloat16).astype(jnp.float32)
+
+    pair = pl.ds(first_ref[0], 2)
+    params = params_ref[pair].reshape(16, 128)
+    upper = rounded(params)
+    high = rounded(squares)
+    middle = rounded(squares - high)
+    share = jnp.concatenate(
+        [
+            held[low_ref[0], pair].reshape(16, 128),
+            upper,
+            params - upper,
+            one_ref[pair].reshape(16, 128),
+            two_ref[pair].reshape(16, 128),
+            high,
+            middle,
+            squares - high - middle,
+            jnp.zeros((5, 128), jnp.float32),
+        ],
+        axis=0,
+    )
+    share_ref[...] = jnp.broadcast_to(share.astype(jnp.bfloat16)[None], share_ref.shape)
+
+
+def expert_grads(first, low, gains, sums, states):
+    experts = gains[0].shape[1]
+    vmem = pl.BlockSpec(memory_space=pltpu.VMEM)
+    smem = pl.BlockSpec(memory_space=pltpu.SMEM)
     return pl.pallas_call(
         expert_kernel,
         out_shape=(
             jax.ShapeDtypeStruct((experts, 8, 128), jnp.float32),
-            jax.ShapeDtypeStruct((shards, 1, 128), jnp.float32),
-        ),
+            jax.ShapeDtypeStruct((16, 88, 128), jnp.bfloat16),
+        ),
+        in_specs=[smem, smem] + [vmem] * 7,
+        out_specs=(vmem, vmem),
+        scratch_shapes=[pltpu.VMEM((2, experts, 8, 128), jnp.float32)],
         compiler_params=PARAMS,
         name="expert_grads",
-    )(data_gain, charge_gain, spin_gain, sums)
-
-
-def adam_kernel(
-    norm_limit,
-    first_ref,
-    square_ref,
-    grad_ref,
-    params_ref,
-    one_ref,
-    two_ref,
-    new_params_ref,
-    new_one_ref,
-    new_two_ref,
-    share_ref,
-):
-    squares = jnp.sum(square_ref[...], axis=0)
-    square_sum = jnp.sum(squares, axis=1, keepdims=True)
-    clip_factor = jnp.minimum(1.0, norm_limit / (jnp.sqrt(square_sum) + 1e-06))
-    clipped = clip_factor[None] * grad_ref[...]
-    new_one = beta_one * one_ref[...] + (1.0 - beta_one) * clipped
-    new_two = beta_two * two_ref[...] + (1.0 - beta_two) * clipped * clipped
+    )(first, low, *gains, sums, *states)
+
+
+def adam_step(clipped, params, moment_one, moment_two):
+    new_one = beta_one * moment_one + (1.0 - beta_one) * clipped
+    new_two = beta_two * moment_two + (1.0 - beta_two) * clipped * clipped
     first_fix = 1.0 - beta_one**STEP
     second_fix = 1.0 - beta_two**STEP
     direction = new_one / first_fix / (jnp.sqrt(new_two / second_fix) + adam_eps)
-    params = params_ref[...]
-    new_params_ref[...] = params - learn_rate * (direction + decay_rate * params)
-    new_one_ref[...] = new_one
-    new_two_ref[...] = new_two
-    mine = new_params_ref[pl.ds(first_ref[0], 2)].reshape(16, 128).astype(jnp.bfloat16)
-    share_ref[...] = jnp.broadcast_to(mine[None], share_ref.shape)
-
-
-def adam_update(first, squares, grads, params, moment_one, moment_two, norm_limit):
-    state = jax.ShapeDtypeStruct(params.shape, jnp.float32)
-    vmem = pl.BlockSpec(memory_space=pltpu.VMEM)
-    return pl.pallas_call(
-        functools.partial(adam_kernel, norm_limit),
-        out_shape=(state, state, state, jax.ShapeDtypeStruct((16, 16, 128), jnp.bfloat16)),
-        in_specs=[pl.BlockSpec(memory_space=pltpu.SMEM)] + [vmem] * 5,
-        out_specs=(vmem,) * 4,
+    new_params = params - learn_rate * (direction + decay_rate * params)
+    return (new_params, new_one, new_two)
+
+
+def weight_kernel(norm_limit, share_ref, clip_ref, weight_ref):
+    part = lambda row, count: share_ref[:, row : row + count, :].astype(jnp.float32)
+    squares = jnp.sum(jnp.sum(part(80, 8), axis=0), axis=0, keepdims=True)
+    square_sum = jnp.sum(squares, axis=1, keepdims=True)
+    clip_factor = jnp.minimum(1.0, norm_limit / (jnp.sqrt(square_sum) + 1e-06))
+    clip_ref[...] = jnp.broadcast_to(clip_factor, clip_ref.shape)
+    for expert in range(2):
+        row = 8 * expert
+        weights = adam_step(
+            clip_factor[None] * part(row, 8),
+            part(16 + row, 8) + part(32 + row, 8),
+            part(48 + row, 8),
+            part(64 + row, 8),
+        )[0].astype(jnp.bfloat16)
+        for copy in range(weight_ref.shape[0]):
+            weight_ref[copy, expert] = weights
+
+
+def expert_weights(share, norm_limit):
+    return pl.pallas_call(
+        functools.partial(weight_kernel, norm_limit),
+        out_shape=(
+            jax.ShapeDtypeStruct((8, 128), jnp.float32),
+            jax.ShapeDtypeStruct((16, 2, 16, 8, 128), jnp.bfloat16),
+        ),
         compiler_params=PARAMS,
+        name="expert_weights",
+    )(share)
+
+
+def adam_kernel(clip_ref, grad_ref, params_ref, one_ref, two_ref, *out_refs):
+    states = (params_ref[...], one_ref[...], two_ref[...])
+    for out_ref, value in zip(out_refs, adam_step(clip_ref[...] * grad_ref[...], *states)):
+        out_ref[...] = value
+
+
+def adam_update(clip, grads, states):
+    size = 4 * grads.size
+    return pl.pallas_call(
+        adam_kernel,
+        out_shape=(jax.ShapeDtypeStruct(grads.shape, jnp.float32),) * 3,
+        compiler_params=PARAMS,
+        cost_estimate=pl.CostEstimate(
+            flops=20 * grads.size, transcendentals=grads.size, bytes_accessed=7 * size
+        ),
         name="adam_update",
-    )(first, squares, grads, params, moment_one, moment_two)
+    )(clip, grads, *states)
+
+
+def exchange(array, axis, groups=None):
+    return lax.all_to_all(array, axis, 0, 0, axis_index_groups=groups, tiled=True)
 
 
 def place_kernel(offset, core_ref, *refs):
@@ -225,10 +287,6 @@
         ),
         name="place_half",
     )(core, half, *held)
-
-
-def exchange(array, axis, groups=None):
-    return lax.all_to_all(array, axis, 0, 0, axis_index_groups=groups, tiled=True)
 
 
 def local(
@@ -250,16 +308,18 @@
     moment_two,
 ):
     channels = node_feat.shape[2] // 2
-    shards, reps = 32, 16
+    reps = 16
     experts, own = params.shape[:2]
     shape = params.shape
     rows = (experts, own * 2, channels)
     place = lax.axis_index("rep")
-    first = jnp.bitwise_and(place, 1) * (experts // 2) + jnp.bitwise_and(place, reps - 2)
     core = jnp.bitwise_and(place, 1)
-    dataset_tag, first, core = lax.optimization_barrier(
-        (dataset_tag, first.reshape(1), core.reshape(1))
-    )
+    first = core * (experts // 2) + jnp.bitwise_and(place, reps - 2)
+    low = jnp.right_shift(lax.axis_index("shard"), 4)
+    dataset_tag, first, core, low = lax.optimization_barrier(
+        (dataset_tag, first.reshape(1), core.reshape(1), low.reshape(1))
+    )
+    states = tuple(array.reshape(rows) for array in (params, moment_one, moment_two))
 
     sums = grouped_sums(
         node_feat,
@@ -285,27 +345,20 @@
     sums = jnp.sum(sums.astype(jnp.float32), axis=0).reshape(16, own, channels)
     sums = exchange(sums, "shard", columns)
     sums = jnp.sum(sums, axis=0)
-    sums = exchange(jnp.broadcast_to(sums[None], (reps, own, channels)), "rep")
-    grads, squares = expert_grads(
-        dataset_gain, charge_gain, spin_gain, sums.reshape(8, 2, own, channels), shards
-    )
-    squares = exchange(squares, "shard")
+    sums = exchange(jnp.broadcast_to(sums[None], (2 * reps, own, channels)), both, planes)
+    gains = (dataset_gain, charge_gain, spin_gain)
+    grads, share = expert_grads(
+        first, low, gains, sums.reshape(2, 8, 2, own, channels), states
+    )
+    share = exchange(share, "shard", columns)
     norm_limit = math.sqrt(experts * 2 * channels * channels)
-    new_params, new_one, new_two, share = adam_update(
-        first,
-        squares,
-        grads,
-        params.reshape(rows),
-        moment_one.reshape(rows),
-        moment_two.reshape(rows),
-        norm_limit,
-    )
-    share = exchange(share, "shard", columns).reshape(16, 2, own * 2, channels)
-    share = jnp.broadcast_to(jnp.swapaxes(share, 0, 1)[None], (16, 2, 16, own * 2, channels))
+    clip, share = expert_weights(share, norm_limit)
     share = exchange(share, both, cores).reshape(8, 2, 2, 16, own * 2, channels)
+    clip, share = lax.optimization_barrier((clip, share))
+    new_params, new_one, new_two = adam_update(clip, grads, states)
     other = lax.ppermute(share, "rep", [(i, i ^ 1) for i in range(reps)])
     full_weights = place_half(1, core, other, place_half(0, core, share))
-    full_weights = full_weights.reshape(experts, shards * own, 2, channels)
+    full_weights = full_weights.reshape(experts, 32 * own, 2, channels)
     return (new_params.reshape(shape), new_one.reshape(shape), new_two.reshape(shape), full_weights)
 
 

time: 120 us -> 113 us (0.942); the launches traced: 120 us -> 112 us
  blocking collectives: 105 us -> 92.5 us
  starting transfers between devices: 5.51 us -> 10.4 us
    all_to_all x6 -> x5, blocking collectives: 105 us -> 92.5 us  [exchange(): lax.all_to_all(array, axis, 0, 0, axis_index_groups=groups, tiled=True)]
    ppermute x1, starting transfers between devices: 5.51 us -> 10.4 us  [local(): other = lax.ppermute(share, 'rep', [(i, i ^ 1) for i in range(reps)])]
  transfers between devices with their start and end apart: 1 -> 1, of which waited for: 1 -> 1; matrix products, arithmetic and copies ran while one was open for 0% -> 0% of each run, Pallas kernels for 1% -> 2%
where the time goes in v5:
time: 113 us; the launch traced here: 112 us
  blocking collectives  92.5 us (82%)
  starting transfers between devices  10.4 us (9%)
  Pallas kernels  7.38 us (7%)
    all_to_all x5, blocking collectives, exchange(): lax.all_to_all(array, axis, 0, 0, axis_index_groups=groups, tiled=True)  92.5 us
    ppermute x1, starting transfers between devices, local(): other = lax.ppermute(share, 'rep', [(i, i ^ 1) for i in range(reps)])  10.4 us
    pallas_call x1, Pallas kernels, grouped_sums(): pl.pallas_call(grouped_kernel, out_shape=jax.ShapeDtypeStruct((32, channe...  3.66 us
  transfers between devices with their start and end apart: 1, of which 1 were waited for; matrix products, arithmetic and copies ran while one was open for 0% of the time, Pallas kernels for 2%

profile of v5, /device:TPU:1, one launch (start us, length us, event | category | flops | bytes accessed | tf_op | source)
XLA Modules:
  0.0 111.7 jit_solution(3357178533204032434)
XLA Ops:
  0.6 0.0 copy-start
  0.6 0.0 copy-start.1
  0.7 0.0 copy-start.2
  0.7 0.0 copy-start.3
  0.7 0.0 copy-start.4
  0.7 0.0 copy-start.5
  0.7 3.7 %grouped_sums.1 = bf16[32,64,128]{2,1,0:T(8,128)(2,1)} custom-call(s32[8]{0:T(128)} %data_tag, s32[8]{0:T(128)} %charge_tag.1, s32[8]{0:T(128)} %spin_tag.1, s32[8]{0:T(128)} %atoms_ref.1, s32[8]{0:T(128)} %edges_ref.1, bf16[8,128,256]{2,1,0:T(8,128)(2,1)} %feat_ref.1, bf16[8,128,256]{2,1,0:T(8,128)(2,1)} %cot_ref.1, f32[8,1536]{1,0:T(8,128)} %length_ref.1, ...), custom_call_target="tpu_custom_call" | custom-call | tf_op jit(solution)/shard_map/grouped_sums/pallas_call | solution.py:96
  4.4 21.9 %all_to_all.25 = bf16[32,64,128]{2,1,0:T(8,128)(2,1)S(1)} all-to-all(bf16[32,64,128]{2,1,0:T(8,128)(2,1)} %grouped_sums.1), channel_id=1, replica_groups={{0,1,2,3,4,5,6,7,8,9,10,11,12,13,14,15,256,257,258,259,260,261,262,263,..., dimensions={0} | all-to-all | bytes 1048576 | tf_op jit(solution)/shard_map/all_to_all | solution.py:252
  26.3 0.1 convert_reduce_fusion
  26.4 24.3 %all_to_all.26 = f32[16,4,128]{2,1,0:T(4,128)S(1)} all-to-all(f32[16,4,128]{2,1,0:T(4,128)S(1)} %bitcast.23), channel_id=1, replica_groups={{0,16,32,48,64,80,96,112,128,144,160,176,192,208,224,240},{256,272,288,..., dimensions={0} | all-to-all | bytes 65536 | tf_op jit(solution)/shard_map/all_to_all | solution.py:252
  50.8 12.3 %all_to_all.27 = f32[32,4,128]{2,1,0:T(4,128)S(1)} all-to-all(f32[32,4,128]{2,1,0:T(4,128)S(1)} %broadcast_in_dim.2), channel_id=1, replica_groups={{0,1,2,3,4,5,6,7,8,9,10,11,12,13,14,15,256,257,258,259,260,261,262,263,..., dimensions={0} | all-to-all | bytes 131072 | tf_op jit(solution)/shard_map/all_to_all | solution.py:252
  63.1 0.0 copy-done
  63.1 0.0 copy-done.1
  63.1 0.0 copy-done.2
  63.1 0.0 copy-done.3
  63.1 0.6 expert_grads.1
  63.8 19.4 %all_to_all.28.share_ref = bf16[16,88,128]{2,1,0:T(8,128)(2,1)S(1)} all-to-all(bf16[16,88,128]{2,1,0:T(8,128)(2,1)S(1)} %get-tuple-element.20), channel_id=1, replica_groups={{0,16,32,48,64,80,96,112,128,144,160,176,192,208,224,240},{256,272,288,..., dimensions={0} | all-to-all | bytes 720896 | tf_op jit(solution)/shard_map/all_to_all | solution.py:252
  83.1 0.3 expert_weights.1
  83.4 14.6 %all_to_all.29 = bf16[16,2,16,8,128]{4,3,2,1,0:T(8,128)(2,1)S(1)} all-to-all(bf16[16,2,16,8,128]{4,3,2,1,0:T(8,128)(2,1)S(1)} %get-tuple-element.22), channel_id=1, replica_groups={{0,256,2,258,4,260,6,262,8,264,10,266,12,268,14,270},{1,257,3,259,5,261..., dimensions={0} | all-to-all | bytes 2097152 | tf_op jit(solution)/shard_map/all_to_all | solution.py:252
  98.0 10.4 %collective-permute-start = (bf16[8,2,2,16,8,128]{5,4,3,2,1,0:T(8,128)(2,1)S(1)}, bf16[8,2,2,16,8,128]{5,4,3,2,1,0:T(8,128)(2,1)S(1)}, u32[]{:S(2)}, u32[]{:S(2)}) collective-permute-start(bf16[8,2,2,16,8,128]{5,4,3,2,1,0:T(8,128)(2,1)S(1)} %bitcast.13), channel_id=1, source_target_pairs={{0,1},{1,0},{2,3},{3,2},{4,5},{5,4},{6,7},{7,6},{8,9},{9,8},{10,11... | collective-permute-start | bytes 3145736 | tf_op jit(solution)/shard_map/ppermute | solution.py:359
  108.4 1.0 place_half.2.refs_1_
  109.4 0.8 adam_update.1
  110.2 0.5 collective-permute-done.refs_0_
  110.7 1.0 place_half.3
  (4 shorter events, 0.0 us)
Async XLA Ops:
  0.6 62.5 %copy-start = (f32[32,4,2,128]{3,2,1,0:T(2,128)S(1)}, f32[32,4,2,128]{3,2,1,0:T(2,128)}, u32[]{:S(2)}) copy-start(f32[32,4,2,128]{3,2,1,0:T(2,128)} %param.29) | copy-start | bytes 393220
  0.6 62.4 %copy-start.1 = (f32[32,4,2,128]{3,2,1,0:T(2,128)S(1)}, f32[32,4,2,128]{3,2,1,0:T(2,128)}, u32[]{:S(2)}) copy-start(f32[32,4,2,128]{3,2,1,0:T(2,128)} %param.30) | copy-start | bytes 393220
  0.7 62.4 %copy-start.2 = (f32[32,4,2,128]{3,2,1,0:T(2,128)S(1)}, f32[32,4,2,128]{3,2,1,0:T(2,128)}, u32[]{:S(2)}) copy-start(f32[32,4,2,128]{3,2,1,0:T(2,128)} %param.31) | copy-start | bytes 393220
  0.7 62.4 %copy-start.3 = (f32[2,32]{1,0:T(2,128)S(1)}, f32[2,32]{1,0:T(2,128)}, u32[]{:S(2)}) copy-start(f32[2,32]{1,0:T(2,128)} %data_ref.1) | copy-start | bytes 772
  0.7 62.4 %copy-start.4 = (f32[2,32]{1,0:T(2,128)S(1)}, f32[2,32]{1,0:T(2,128)}, u32[]{:S(2)}) copy-start(f32[2,32]{1,0:T(2,128)} %charge_ref.1) | copy-start | bytes 772
  0.7 62.4 %copy-start.5 = (f32[2,32]{1,0:T(2,128)S(1)}, f32[2,32]{1,0:T(2,128)}, u32[]{:S(2)}) copy-start(f32[2,32]{1,0:T(2,128)} %spin_ref.1) | copy-start | bytes 772
  98.0 12.7 %collective-permute-start = (bf16[8,2,2,16,8,128]{5,4,3,2,1,0:T(8,128)(2,1)S(1)}, bf16[8,2,2,16,8,128]{5,4,3,2,1,0:T(8,128)(2,1)S(1)}, u32[]{:S(2)}, u32[]{:S(2)}) collective-permute-start(bf16[8,2,2,16,8,128]{5,4,3,2,1,0:T(8,128)(2,1)S(1)} %bitcast.13), channel_id=1, source_target_pairs={{0,1},{1,0},{2,3},{3,2},{4,5},{5,4},{6,7},{7,6},{8,9},{9,8},{10,11... | collective-permute-start | bytes 3145736 | tf_op jit(solution)/shard_map/ppermute | solution.py:359

commit v6 on v5

--- a/solution.py
+++ b/solution.py
@@ -152,19 +152,22 @@
     pair = pl.ds(first_ref[0], 2)
     params = params_ref[pair].reshape(16, 128)
     upper = rounded(params)
-    high = rounded(squares)
-    middle = rounded(squares - high)
+    lower = params - upper
+    square_sum = jnp.broadcast_to(jnp.sum(squares, axis=1, keepdims=True), lower.shape)
+    high = rounded(square_sum)
+    middle = rounded(square_sum - high)
+    rows = lax.broadcasted_iota(jnp.int32, lower.shape, 0)
+    lanes = lax.broadcasted_iota(jnp.int32, lower.shape, 1)
+    terms = jnp.where(lanes == 2, square_sum - high - middle, 0.0)
+    terms = jnp.where(lanes == 1, middle, terms)
+    terms = jnp.where(lanes == 0, high, terms)
     share = jnp.concatenate(
         [
             held[low_ref[0], pair].reshape(16, 128),
             upper,
-            params - upper,
+            jnp.where(rows == 15, terms, lower),
             one_ref[pair].reshape(16, 128),
             two_ref[pair].reshape(16, 128),
-            high,
-            middle,
-            squares - high - middle,
-            jnp.zeros((5, 128), jnp.float32),
         ],
         axis=0,
     )
@@ -179,7 +182,7 @@
         expert_kernel,
         out_shape=(
             jax.ShapeDtypeStruct((experts, 8, 128), jnp.float32),
-            jax.ShapeDtypeStruct((16, 88, 128), jnp.bfloat16),
+            jax.ShapeDtypeStruct((16, 80, 128), jnp.bfloat16),
         ),
         in_specs=[smem, smem] + [vmem] * 7,
         out_specs=(vmem, vmem),
@@ -201,15 +204,19 @@
 
 def weight_kernel(norm_limit, share_ref, clip_ref, weight_ref):
     part = lambda row, count: share_ref[:, row : row + count, :].astype(jnp.float32)
-    squares = jnp.sum(jnp.sum(part(80, 8), axis=0), axis=0, keepdims=True)
-    square_sum = jnp.sum(squares, axis=1, keepdims=True)
+    row_ids = lax.broadcasted_iota(jnp.int32, (16, 8, 128), 1)
+    squares = jnp.sum(jnp.where(row_ids == 7, part(40, 8), 0.0), axis=0)
+    square_sum = jnp.sum(jnp.sum(squares, axis=0, keepdims=True), axis=1, keepdims=True)
     clip_factor = jnp.minimum(1.0, norm_limit / (jnp.sqrt(square_sum) + 1e-06))
     clip_ref[...] = jnp.broadcast_to(clip_factor, clip_ref.shape)
     for expert in range(2):
         row = 8 * expert
+        lower = part(32 + row, 8)
+        if expert == 1:
+            lower = jnp.where(row_ids == 7, 0.0, lower)
         weights = adam_step(
             clip_factor[None] * part(row, 8),
-            part(16 + row, 8) + part(32 + row, 8),
+            part(16 + row, 8) + lower,
             part(48 + row, 8),
             part(64 + row, 8),
         )[0].astype(jnp.bfloat16)

time: 113 us -> 112 us (level)
    all_to_all x5, blocking collectives: 92.5 us -> 91.4 us  [exchange(): lax.all_to_all(array, axis, 0, 0, axis_index_groups=groups, tiled=True)]
where the time goes in v6:
time: 112 us; the launch traced here: 110 us
  blocking collectives  91.4 us (82%)
  starting transfers between devices  9.7 us (9%)
  Pallas kernels  7.46 us (7%)
    all_to_all x5, blocking collectives, exchange(): lax.all_to_all(array, axis, 0, 0, axis_index_groups=groups, tiled=True)  91.4 us
    ppermute x1, starting transfers between devices, local(): other = lax.ppermute(share, 'rep', [(i, i ^ 1) for i in range(reps)])  9.7 us
    pallas_call x1, Pallas kernels, grouped_sums(): pl.pallas_call(grouped_kernel, out_shape=jax.ShapeDtypeStruct((32, channe...  3.66 us
  transfers between devices with their start and end apart: 1, of which 1 were waited for; matrix products, arithmetic and copies ran while one was open for 0% of the time, Pallas kernels for 2%

profile of v6, /device:TPU:1, one launch (start us, length us, event | category | flops | bytes accessed | tf_op | source)
XLA Modules:
  0.0 109.9 jit_solution(3383379518158068791)
XLA Ops:
  0.6 0.0 copy-start
  0.6 0.0 copy-start.1
  0.7 0.0 copy-start.2
  0.7 0.0 copy-start.3
  0.7 0.0 copy-start.4
  0.7 0.0 copy-start.5
  0.7 3.7 %grouped_sums.1 = bf16[32,64,128]{2,1,0:T(8,128)(2,1)} custom-call(s32[8]{0:T(128)} %data_tag, s32[8]{0:T(128)} %charge_tag.1, s32[8]{0:T(128)} %spin_tag.1, s32[8]{0:T(128)} %atoms_ref.1, s32[8]{0:T(128)} %edges_ref.1, bf16[8,128,256]{2,1,0:T(8,128)(2,1)} %feat_ref.1, bf16[8,128,256]{2,1,0:T(8,128)(2,1)} %cot_ref.1, f32[8,1536]{1,0:T(8,128)} %length_ref.1, ...), custom_call_target="tpu_custom_call" | custom-call | tf_op jit(solution)/shard_map/grouped_sums/pallas_call | solution.py:96
  4.4 21.9 %all_to_all.25 = bf16[32,64,128]{2,1,0:T(8,128)(2,1)S(1)} all-to-all(bf16[32,64,128]{2,1,0:T(8,128)(2,1)} %grouped_sums.1), channel_id=1, replica_groups={{0,1,2,3,4,5,6,7,8,9,10,11,12,13,14,15,256,257,258,259,260,261,262,263,..., dimensions={0} | all-to-all | bytes 1048576 | tf_op jit(solution)/shard_map/all_to_all | solution.py:259
  26.3 0.1 convert_reduce_fusion
  26.4 24.3 %all_to_all.26 = f32[16,4,128]{2,1,0:T(4,128)S(1)} all-to-all(f32[16,4,128]{2,1,0:T(4,128)S(1)} %bitcast.23), channel_id=1, replica_groups={{0,16,32,48,64,80,96,112,128,144,160,176,192,208,224,240},{256,272,288,..., dimensions={0} | all-to-all | bytes 65536 | tf_op jit(solution)/shard_map/all_to_all | solution.py:259
  50.8 12.3 %all_to_all.27 = f32[32,4,128]{2,1,0:T(4,128)S(1)} all-to-all(f32[32,4,128]{2,1,0:T(4,128)S(1)} %broadcast_in_dim.2), channel_id=1, replica_groups={{0,1,2,3,4,5,6,7,8,9,10,11,12,13,14,15,256,257,258,259,260,261,262,263,..., dimensions={0} | all-to-all | bytes 131072 | tf_op jit(solution)/shard_map/all_to_all | solution.py:259
  63.1 0.0 copy-done
  63.1 0.0 copy-done.1
  63.1 0.0 copy-done.2
  63.1 0.0 copy-done.3
  63.1 0.7 expert_grads.1
  63.8 18.2 %all_to_all.28.share_ref = bf16[16,80,128]{2,1,0:T(8,128)(2,1)S(1)} all-to-all(bf16[16,80,128]{2,1,0:T(8,128)(2,1)S(1)} %get-tuple-element.20), channel_id=1, replica_groups={{0,16,32,48,64,80,96,112,128,144,160,176,192,208,224,240},{256,272,288,..., dimensions={0} | all-to-all | bytes 655360 | tf_op jit(solution)/shard_map/all_to_all | solution.py:259
  82.1 0.3 expert_weights.1
  82.4 14.6 %all_to_all.29 = bf16[16,2,16,8,128]{4,3,2,1,0:T(8,128)(2,1)S(1)} all-to-all(bf16[16,2,16,8,128]{4,3,2,1,0:T(8,128)(2,1)S(1)} %get-tuple-element.22), channel_id=1, replica_groups={{0,256,2,258,4,260,6,262,8,264,10,266,12,268,14,270},{1,257,3,259,5,261..., dimensions={0} | all-to-all | bytes 2097152 | tf_op jit(solution)/shard_map/all_to_all | solution.py:259
  96.9 9.7 %collective-permute-start = (bf16[8,2,2,16,8,128]{5,4,3,2,1,0:T(8,128)(2,1)S(1)}, bf16[8,2,2,16,8,128]{5,4,3,2,1,0:T(8,128)(2,1)S(1)}, u32[]{:S(2)}, u32[]{:S(2)}) collective-permute-start(bf16[8,2,2,16,8,128]{5,4,3,2,1,0:T(8,128)(2,1)S(1)} %bitcast.13), channel_id=1, source_target_pairs={{0,1},{1,0},{2,3},{3,2},{4,5},{5,4},{6,7},{7,6},{8,9},{9,8},{10,11... | collective-permute-start | bytes 3145736 | tf_op jit(solution)/shard_map/ppermute | solution.py:366
  106.7 1.0 place_half.2.refs_1_
  107.7 0.8 adam_update.1
  108.5 0.5 collective-permute-done.refs_0_
  108.9 1.0 place_half.3
  (4 shorter events, 0.0 us)
Async XLA Ops:
  0.6 62.5 %copy-start = (f32[32,4,2,128]{3,2,1,0:T(2,128)S(1)}, f32[32,4,2,128]{3,2,1,0:T(2,128)}, u32[]{:S(2)}) copy-start(f32[32,4,2,128]{3,2,1,0:T(2,128)} %param.29) | copy-start | bytes 393220
  0.6 62.4 %copy-start.1 = (f32[32,4,2,128]{3,2,1,0:T(2,128)S(1)}, f32[32,4,2,128]{3,2,1,0:T(2,128)}, u32[]{:S(2)}) copy-start(f32[32,4,2,128]{3,2,1,0:T(2,128)} %param.30) | copy-start | bytes 393220
  0.7 62.4 %copy-start.2 = (f32[32,4,2,128]{3,2,1,0:T(2,128)S(1)}, f32[32,4,2,128]{3,2,1,0:T(2,128)}, u32[]{:S(2)}) copy-start(f32[32,4,2,128]{3,2,1,0:T(2,128)} %param.31) | copy-start | bytes 393220
  0.7 62.4 %copy-start.3 = (f32[2,32]{1,0:T(2,128)S(1)}, f32[2,32]{1,0:T(2,128)}, u32[]{:S(2)}) copy-start(f32[2,32]{1,0:T(2,128)} %data_ref.1) | copy-start | bytes 772
  0.7 62.4 %copy-start.4 = (f32[2,32]{1,0:T(2,128)S(1)}, f32[2,32]{1,0:T(2,128)}, u32[]{:S(2)}) copy-start(f32[2,32]{1,0:T(2,128)} %charge_ref.1) | copy-start | bytes 772
  0.7 62.4 %copy-start.5 = (f32[2,32]{1,0:T(2,128)S(1)}, f32[2,32]{1,0:T(2,128)}, u32[]{:S(2)}) copy-start(f32[2,32]{1,0:T(2,128)} %spin_ref.1) | copy-start | bytes 772
  96.9 12.0 %collective-permute-start = (bf16[8,2,2,16,8,128]{5,4,3,2,1,0:T(8,128)(2,1)S(1)}, bf16[8,2,2,16,8,128]{5,4,3,2,1,0:T(8,128)(2,1)S(1)}, u32[]{:S(2)}, u32[]{:S(2)}) collective-permute-start(bf16[8,2,2,16,8,128]{5,4,3,2,1,0:T(8,128)(2,1)S(1)} %bitcast.13), channel_id=1, source_target_pairs={{0,1},{1,0},{2,3},{3,2},{4,5},{5,4},{6,7},{7,6},{8,9},{9,8},{10,11... | collective-permute-start | bytes 3145736 | tf_op jit(solution)/shard_map/ppermute | solution.py:366

commit v7 on v6

--- a/solution.py
+++ b/solution.py
@@ -105,6 +105,31 @@
     )(data_tag, charge_tag, spin_tag, atoms, edges, feat, cot, length, source, target)
 
 
+def rounded(value):
+    return value.astype(jnp.bfloat16).astype(jnp.float32)
+
+
+def scatter_kernel(first_ref, sums_ref, params_ref, out_ref):
+    total = jnp.sum(sums_ref[...].astype(jnp.float32), axis=0)
+    high = rounded(total)
+    params = params_ref[pl.ds(first_ref[0], 1)]
+    lower = jnp.broadcast_to(params - rounded(params), (16, 8, 128))
+    parts = [high.reshape(16, 4, 128), (total - high).reshape(16, 4, 128), lower]
+    out_ref[...] = jnp.concatenate(parts, axis=1).astype(jnp.bfloat16)
+
+
+def scatter_message(first, sums, params):
+    vmem = pl.BlockSpec(memory_space=pltpu.VMEM)
+    return pl.pallas_call(
+        scatter_kernel,
+        out_shape=jax.ShapeDtypeStruct((16, 16, 128), jnp.bfloat16),
+        in_specs=[pl.BlockSpec(memory_space=pltpu.SMEM), vmem, vmem],
+        out_specs=vmem,
+        compiler_params=PARAMS,
+        name="scatter_message",
+    )(first, sums, params)
+
+
 def expert_kernel(
     first_ref,
     low_ref,
@@ -146,9 +171,6 @@
                 squares = term if squares is None else squares + term
     grad_ref[...] = held[low_ref[0]]
 
-    def rounded(value):
-        return value.astype(jnp.bfloat16).astype(jnp.float32)
-
     pair = pl.ds(first_ref[0], 2)
     params = params_ref[pair].reshape(16, 128)
     upper = rounded(params)
@@ -165,7 +187,7 @@
         [
             held[low_ref[0], pair].reshape(16, 128),
             upper,
-            jnp.where(rows == 15, terms, lower),
+            jnp.where(rows == 15, terms, lower)[8:],
             one_ref[pair].reshape(16, 128),
             two_ref[pair].reshape(16, 128),
         ],
@@ -182,7 +204,7 @@
         expert_kernel,
         out_shape=(
             jax.ShapeDtypeStruct((experts, 8, 128), jnp.float32),
-            jax.ShapeDtypeStruct((16, 80, 128), jnp.bfloat16),
+            jax.ShapeDtypeStruct((16, 72, 128), jnp.bfloat16),
         ),
         in_specs=[smem, smem] + [vmem] * 7,
         out_specs=(vmem, vmem),
@@ -202,29 +224,30 @@
     return (new_params, new_one, new_two)
 
 
-def weight_kernel(norm_limit, share_ref, clip_ref, weight_ref):
+def weight_kernel(norm_limit, share_ref, early_ref, clip_ref, weight_ref):
     part = lambda row, count: share_ref[:, row : row + count, :].astype(jnp.float32)
     row_ids = lax.broadcasted_iota(jnp.int32, (16, 8, 128), 1)
-    squares = jnp.sum(jnp.where(row_ids == 7, part(40, 8), 0.0), axis=0)
+    squares = jnp.sum(jnp.where(row_ids == 7, part(32, 8), 0.0), axis=0)
     square_sum = jnp.sum(jnp.sum(squares, axis=0, keepdims=True), axis=1, keepdims=True)
     clip_factor = jnp.minimum(1.0, norm_limit / (jnp.sqrt(square_sum) + 1e-06))
     clip_ref[...] = jnp.broadcast_to(clip_factor, clip_ref.shape)
     for expert in range(2):
         row = 8 * expert
-        lower = part(32 + row, 8)
-        if expert == 1:
-            lower = jnp.where(row_ids == 7, 0.0, lower)
+        if expert == 0:
+            lower = early_ref[:, 8:16, :].astype(jnp.float32)
+        else:
+            lower = jnp.where(row_ids == 7, 0.0, part(32, 8))
         weights = adam_step(
             clip_factor[None] * part(row, 8),
             part(16 + row, 8) + lower,
-            part(48 + row, 8),
-            part(64 + row, 8),
+            part(40 + row, 8),
+            part(56 + row, 8),
         )[0].astype(jnp.bfloat16)
         for copy in range(weight_ref.shape[0]):
             weight_ref[copy, expert] = weights
 
 
-def expert_weights(share, norm_limit):
+def expert_weights(share, early, norm_limit):
     return pl.pallas_call(
         functools.partial(weight_kernel, norm_limit),
         out_shape=(
@@ -233,7 +256,7 @@
         ),
         compiler_params=PARAMS,
         name="expert_weights",
-    )(share)
+    )(share, early)
 
 
 def adam_kernel(clip_ref, grad_ref, params_ref, one_ref, two_ref, *out_refs):
@@ -349,9 +372,9 @@
         for core in range(2)
     ]
     sums = exchange(sums, both, planes)
-    sums = jnp.sum(sums.astype(jnp.float32), axis=0).reshape(16, own, channels)
-    sums = exchange(sums, "shard", columns)
-    sums = jnp.sum(sums, axis=0)
+    early = exchange(scatter_message(first, sums, states[0]), "shard", columns)
+    sums = jnp.sum(early[:, : 2 * own].astype(jnp.float32), axis=0)
+    sums = sums[:own] + sums[own:]
     sums = exchange(jnp.broadcast_to(sums[None], (2 * reps, own, channels)), both, planes)
     gains = (dataset_gain, charge_gain, spin_gain)
     grads, share = expert_grads(
@@ -359,7 +382,7 @@
     )
     share = exchange(share, "shard", columns)
     norm_limit = math.sqrt(experts * 2 * channels * channels)
-    clip, share = expert_weights(share, norm_limit)
+    clip, share = expert_weights(share, early, norm_limit)
     share = exchange(share, both, cores).reshape(8, 2, 2, 16, own * 2, channels)
     clip, share = lax.optimization_barrier((clip, share))
     new_params, new_one, new_two = adam_update(clip, grads, states)

time: 112 us -> 111 us (level)
  no operation moved by 1% of the time
where the time goes in v7:
time: 111 us; the launch traced here: 109 us
  blocking collectives  90.6 us (82%)
  starting transfers between devices  9.49 us (9%)
  Pallas kernels  7.56 us (7%)
    all_to_all x5, blocking collectives, exchange(): lax.all_to_all(array, axis, 0, 0, axis_index_groups=groups, tiled=True)  90.6 us
    ppermute x1, starting transfers between devices, local(): other = lax.ppermute(share, 'rep', [(i, i ^ 1) for i in range(reps)])  9.49 us
    pallas_call x1, Pallas kernels, grouped_sums(): pl.pallas_call(grouped_kernel, out_shape=jax.ShapeDtypeStruct((32, channe...  3.66 us
  transfers between devices with their start and end apart: 1, of which 1 were waited for; matrix products, arithmetic and copies ran while one was open for 0% of the time, Pallas kernels for 2%

profile of v7, /device:TPU:1, one launch (start us, length us, event | category | flops | bytes accessed | tf_op | source)
XLA Modules:
  0.0 108.9 jit_solution(15709190137909021249)
XLA Ops:
  0.6 0.0 copy-start
  0.6 0.0 copy-start.1
  0.7 0.0 copy-start.2
  0.7 0.0 copy-start.3
  0.7 0.0 copy-start.4
  0.7 0.0 copy-start.5
  0.7 3.7 %grouped_sums.1 = bf16[32,64,128]{2,1,0:T(8,128)(2,1)} custom-call(s32[8]{0:T(128)} %data_tag, s32[8]{0:T(128)} %charge_tag.1, s32[8]{0:T(128)} %spin_tag.1, s32[8]{0:T(128)} %atoms_ref.1, s32[8]{0:T(128)} %edges_ref.1, bf16[8,128,256]{2,1,0:T(8,128)(2,1)} %feat_ref.1, bf16[8,128,256]{2,1,0:T(8,128)(2,1)} %cot_ref.1, f32[8,1536]{1,0:T(8,128)} %length_ref.1, ...), custom_call_target="tpu_custom_call" | custom-call | tf_op jit(solution)/shard_map/grouped_sums/pallas_call | solution.py:96
  4.4 21.9 %all_to_all.25.sums_ref = bf16[32,64,128]{2,1,0:T(8,128)(2,1)S(1)} all-to-all(bf16[32,64,128]{2,1,0:T(8,128)(2,1)} %grouped_sums.1), channel_id=1, replica_groups={{0,1,2,3,4,5,6,7,8,9,10,11,12,13,14,15,256,257,258,259,260,261,262,263,..., dimensions={0} | all-to-all | bytes 1048576 | tf_op jit(solution)/shard_map/all_to_all | solution.py:282
  26.3 0.0 copy-done
  26.3 0.1 scatter_message.1
  26.4 24.4 %all_to_all.26.early_ref = bf16[16,16,128]{2,1,0:T(8,128)(2,1)S(1)} all-to-all(bf16[16,16,128]{2,1,0:T(8,128)(2,1)S(1)} %scatter_message.1), channel_id=1, replica_groups={{0,16,32,48,64,80,96,112,128,144,160,176,192,208,224,240},{256,272,288,..., dimensions={0} | all-to-all | bytes 131072 | tf_op jit(solution)/shard_map/all_to_all | solution.py:282
  50.9 12.6 %all_to_all.27 = f32[32,4,128]{2,1,0:T(4,128)S(1)} all-to-all(f32[32,4,128]{2,1,0:T(4,128)S(1)} %broadcast_in_dim.2), channel_id=1, replica_groups={{0,1,2,3,4,5,6,7,8,9,10,11,12,13,14,15,256,257,258,259,260,261,262,263,..., dimensions={0} | all-to-all | bytes 131072 | tf_op jit(solution)/shard_map/all_to_all | solution.py:282
  63.5 0.0 copy-done.3
  63.5 0.0 copy-done.4
  63.5 0.0 copy-done.5
  63.5 0.7 expert_grads.1
  64.2 17.0 %all_to_all.28.share_ref = bf16[16,72,128]{2,1,0:T(8,128)(2,1)S(1)} all-to-all(bf16[16,72,128]{2,1,0:T(8,128)(2,1)S(1)} %get-tuple-element.20), channel_id=1, replica_groups={{0,16,32,48,64,80,96,112,128,144,160,176,192,208,224,240},{256,272,288,..., dimensions={0} | all-to-all | bytes 589824 | tf_op jit(solution)/shard_map/all_to_all | solution.py:282
  81.2 0.3 expert_weights.1
  81.5 14.6 %all_to_all.29 = bf16[16,2,16,8,128]{4,3,2,1,0:T(8,128)(2,1)S(1)} all-to-all(bf16[16,2,16,8,128]{4,3,2,1,0:T(8,128)(2,1)S(1)} %get-tuple-element.22), channel_id=1, replica_groups={{0,256,2,258,4,260,6,262,8,264,10,266,12,268,14,270},{1,257,3,259,5,261..., dimensions={0} | all-to-all | bytes 2097152 | tf_op jit(solution)/shard_map/all_to_all | solution.py:282
  96.1 9.5 %collective-permute-start = (bf16[8,2,2,16,8,128]{5,4,3,2,1,0:T(8,128)(2,1)S(1)}, bf16[8,2,2,16,8,128]{5,4,3,2,1,0:T(8,128)(2,1)S(1)}, u32[]{:S(2)}, u32[]{:S(2)}) collective-permute-start(bf16[8,2,2,16,8,128]{5,4,3,2,1,0:T(8,128)(2,1)S(1)} %bitcast.12), channel_id=1, source_target_pairs={{0,1},{1,0},{2,3},{3,2},{4,5},{5,4},{6,7},{7,6},{8,9},{9,8},{10,11... | collective-permute-start | bytes 3145736 | tf_op jit(solution)/shard_map/ppermute | solution.py:389
  105.6 1.0 place_half.2.refs_1_
  106.6 0.8 adam_update.1
  107.4 0.5 collective-permute-done.refs_0_
  107.9 1.0 place_half.3
  (5 shorter events, 0.0 us)
Async XLA Ops:
  0.6 25.7 %copy-start = (f32[32,4,2,128]{3,2,1,0:T(2,128)S(1)}, f32[32,4,2,128]{3,2,1,0:T(2,128)}, u32[]{:S(2)}) copy-start(f32[32,4,2,128]{3,2,1,0:T(2,128)} %param.29) | copy-start | bytes 393220
  0.6 62.8 %copy-start.1 = (f32[32,4,2,128]{3,2,1,0:T(2,128)S(1)}, f32[32,4,2,128]{3,2,1,0:T(2,128)}, u32[]{:S(2)}) copy-start(f32[32,4,2,128]{3,2,1,0:T(2,128)} %param.30) | copy-start | bytes 393220
  0.7 62.8 %copy-start.2 = (f32[32,4,2,128]{3,2,1,0:T(2,128)S(1)}, f32[32,4,2,128]{3,2,1,0:T(2,128)}, u32[]{:S(2)}) copy-start(f32[32,4,2,128]{3,2,1,0:T(2,128)} %param.31) | copy-start | bytes 393220
  0.7 62.8 %copy-start.3 = (f32[2,32]{1,0:T(2,128)S(1)}, f32[2,32]{1,0:T(2,128)}, u32[]{:S(2)}) copy-start(f32[2,32]{1,0:T(2,128)} %data_ref.1) | copy-start | bytes 772
  0.7 62.8 %copy-start.4 = (f32[2,32]{1,0:T(2,128)S(1)}, f32[2,32]{1,0:T(2,128)}, u32[]{:S(2)}) copy-start(f32[2,32]{1,0:T(2,128)} %charge_ref.1) | copy-start | bytes 772
  0.7 62.8 %copy-start.5 = (f32[2,32]{1,0:T(2,128)S(1)}, f32[2,32]{1,0:T(2,128)}, u32[]{:S(2)}) copy-start(f32[2,32]{1,0:T(2,128)} %spin_ref.1) | copy-start | bytes 772
  96.1 11.8 %collective-permute-start = (bf16[8,2,2,16,8,128]{5,4,3,2,1,0:T(8,128)(2,1)S(1)}, bf16[8,2,2,16,8,128]{5,4,3,2,1,0:T(8,128)(2,1)S(1)}, u32[]{:S(2)}, u32[]{:S(2)}) collective-permute-start(bf16[8,2,2,16,8,128]{5,4,3,2,1,0:T(8,128)(2,1)S(1)} %bitcast.12), channel_id=1, source_target_pairs={{0,1},{1,0},{2,3},{3,2},{4,5},{5,4},{6,7},{7,6},{8,9},{9,8},{10,11... | collective-permute-start | bytes 3145736 | tf_op jit(solution)/shard_map/ppermute | solution.py:389

commit v8 on v7

--- a/solution.py
+++ b/solution.py
@@ -287,7 +287,7 @@
     side = jnp.bitwise_xor(core_ref[0], offset)
     copies = [
         pltpu.make_async_copy(
-            half_ref.at[:, low, expert], out_ref.at[side, :, expert, low], sems.at[2 * low + expert]
+            half_ref.at[low, :, expert], out_ref.at[side, :, expert, low], sems.at[2 * low + expert]
         )
         for low in range(2)
         for expert in range(2)
@@ -367,7 +367,7 @@
     planes = [[(16 * low + z) * reps + i for low in range(2) for i in range(reps)] for z in range(16)]
     columns = [[16 * low + z for z in range(16)] for low in range(2)]
     cores = [
-        [(16 * low + z) * reps + 2 * i + core for i in range(8) for low in range(2)]
+        [(16 * low + z) * reps + 2 * i + core for low in range(2) for i in range(8)]
         for z in range(16)
         for core in range(2)
     ]
@@ -383,7 +383,7 @@
     share = exchange(share, "shard", columns)
     norm_limit = math.sqrt(experts * 2 * channels * channels)
     clip, share = expert_weights(share, early, norm_limit)
-    share = exchange(share, both, cores).reshape(8, 2, 2, 16, own * 2, channels)
+    share = exchange(share, both, cores).reshape(2, 8, 2, 16, own * 2, channels)
     clip, share = lax.optimization_barrier((clip, share))
     new_params, new_one, new_two = adam_update(clip, grads, states)
     other = lax.ppermute(share, "rep", [(i, i ^ 1) for i in range(reps)])

time: 111 us -> 111 us (level)
  no operation moved by 1% of the time
where the time goes in v8:
time: 111 us; the launch traced here: 109 us
  blocking collectives  90.6 us (82%)
  starting transfers between devices  9.39 us (8%)
  Pallas kernels  7.56 us (7%)
    all_to_all x5, blocking collectives, exchange(): lax.all_to_all(array, axis, 0, 0, axis_index_groups=groups, tiled=True)  90.6 us
    ppermute x1, starting transfers between devices, local(): other = lax.ppermute(share, 'rep', [(i, i ^ 1) for i in range(reps)])  9.39 us
    pallas_call x1, Pallas kernels, grouped_sums(): pl.pallas_call(grouped_kernel, out_shape=jax.ShapeDtypeStruct((32, channe...  3.66 us
  transfers between devices with their start and end apart: 1, of which 1 were waited for; matrix products, arithmetic and copies ran while one was open for 0% of the time, Pallas kernels for 2%

profile of v8, /device:TPU:1, one launch (start us, length us, event | category | flops | bytes accessed | tf_op | source)
XLA Modules:
  0.0 108.8 jit_solution(13452796493284022914)
XLA Ops:
  0.6 0.0 copy-start
  0.6 0.0 copy-start.1
  0.7 0.0 copy-start.2
  0.7 0.0 copy-start.3
  0.7 0.0 copy-start.4
  0.7 0.0 copy-start.5
  0.7 3.7 %grouped_sums.1 = bf16[32,64,128]{2,1,0:T(8,128)(2,1)} custom-call(s32[8]{0:T(128)} %data_tag, s32[8]{0:T(128)} %charge_tag.1, s32[8]{0:T(128)} %spin_tag.1, s32[8]{0:T(128)} %atoms_ref.1, s32[8]{0:T(128)} %edges_ref.1, bf16[8,128,256]{2,1,0:T(8,128)(2,1)} %feat_ref.1, bf16[8,128,256]{2,1,0:T(8,128)(2,1)} %cot_ref.1, f32[8,1536]{1,0:T(8,128)} %length_ref.1, ...), custom_call_target="tpu_custom_call" | custom-call | tf_op jit(solution)/shard_map/grouped_sums/pallas_call | solution.py:96
  4.4 21.9 %all_to_all.25.sums_ref = bf16[32,64,128]{2,1,0:T(8,128)(2,1)S(1)} all-to-all(bf16[32,64,128]{2,1,0:T(8,128)(2,1)} %grouped_sums.1), channel_id=1, replica_groups={{0,1,2,3,4,5,6,7,8,9,10,11,12,13,14,15,256,257,258,259,260,261,262,263,..., dimensions={0} | all-to-all | bytes 1048576 | tf_op jit(solution)/shard_map/all_to_all | solution.py:282
  26.3 0.0 copy-done
  26.3 0.1 scatter_message.1
  26.4 24.4 %all_to_all.26.early_ref = bf16[16,16,128]{2,1,0:T(8,128)(2,1)S(1)} all-to-all(bf16[16,16,128]{2,1,0:T(8,128)(2,1)S(1)} %scatter_message.1), channel_id=1, replica_groups={{0,16,32,48,64,80,96,112,128,144,160,176,192,208,224,240},{256,272,288,..., dimensions={0} | all-to-all | bytes 131072 | tf_op jit(solution)/shard_map/all_to_all | solution.py:282
  50.9 12.6 %all_to_all.27 = f32[32,4,128]{2,1,0:T(4,128)S(1)} all-to-all(f32[32,4,128]{2,1,0:T(4,128)S(1)} %broadcast_in_dim.2), channel_id=1, replica_groups={{0,1,2,3,4,5,6,7,8,9,10,11,12,13,14,15,256,257,258,259,260,261,262,263,..., dimensions={0} | all-to-all | bytes 131072 | tf_op jit(solution)/shard_map/all_to_all | solution.py:282
  63.5 0.0 copy-done.1
  63.5 0.0 copy-done.2
  63.5 0.0 copy-done.3
  63.5 0.7 expert_grads.1
  64.2 17.0 %all_to_all.28.share_ref = bf16[16,72,128]{2,1,0:T(8,128)(2,1)S(1)} all-to-all(bf16[16,72,128]{2,1,0:T(8,128)(2,1)S(1)} %get-tuple-element.20), channel_id=1, replica_groups={{0,16,32,48,64,80,96,112,128,144,160,176,192,208,224,240},{256,272,288,..., dimensions={0} | all-to-all | bytes 589824 | tf_op jit(solution)/shard_map/all_to_all | solution.py:282
  81.2 0.3 expert_weights.1
  81.5 14.6 %all_to_all.29 = bf16[16,2,16,8,128]{4,3,2,1,0:T(8,128)(2,1)S(1)} all-to-all(bf16[16,2,16,8,128]{4,3,2,1,0:T(8,128)(2,1)S(1)} %get-tuple-element.22), channel_id=1, replica_groups={{0,2,4,6,8,10,12,14,256,258,260,262,264,266,268,270},{1,3,5,7,9,11,13,1..., dimensions={0} | all-to-all | bytes 2097152 | tf_op jit(solution)/shard_map/all_to_all | solution.py:282
  96.2 9.4 %collective-permute-start = (bf16[2,8,2,16,8,128]{5,4,3,2,1,0:T(8,128)(2,1)S(1)}, bf16[2,8,2,16,8,128]{5,4,3,2,1,0:T(8,128)(2,1)S(1)}, u32[]{:S(2)}, u32[]{:S(2)}) collective-permute-start(bf16[2,8,2,16,8,128]{5,4,3,2,1,0:T(8,128)(2,1)S(1)} %bitcast.12), channel_id=1, source_target_pairs={{0,1},{1,0},{2,3},{3,2},{4,5},{5,4},{6,7},{7,6},{8,9},{9,8},{10,11... | collective-permute-start | bytes 3145736 | tf_op jit(solution)/shard_map/ppermute | solution.py:389
  105.6 1.0 place_half.2.refs_1_
  106.6 0.8 adam_update.1
  107.4 0.5 collective-permute-done.refs_0_
  107.8 1.0 place_half.3
  (5 shorter events, 0.0 us)
Async XLA Ops:
  0.6 25.7 %copy-start = (f32[32,4,2,128]{3,2,1,0:T(2,128)S(1)}, f32[32,4,2,128]{3,2,1,0:T(2,128)}, u32[]{:S(2)}) copy-start(f32[32,4,2,128]{3,2,1,0:T(2,128)} %param.29) | copy-start | bytes 393220
  0.6 62.8 %copy-start.1 = (f32[32,4,2,128]{3,2,1,0:T(2,128)S(1)}, f32[32,4,2,128]{3,2,1,0:T(2,128)}, u32[]{:S(2)}) copy-start(f32[32,4,2,128]{3,2,1,0:T(2,128)} %param.30) | copy-start | bytes 393220
  0.7 62.8 %copy-start.2 = (f32[32,4,2,128]{3,2,1,0:T(2,128)S(1)}, f32[32,4,2,128]{3,2,1,0:T(2,128)}, u32[]{:S(2)}) copy-start(f32[32,4,2,128]{3,2,1,0:T(2,128)} %param.31) | copy-start | bytes 393220
  0.7 62.8 %copy-start.3 = (f32[2,32]{1,0:T(2,128)S(1)}, f32[2,32]{1,0:T(2,128)}, u32[]{:S(2)}) copy-start(f32[2,32]{1,0:T(2,128)} %data_ref.1) | copy-start | bytes 772
  0.7 62.8 %copy-start.4 = (f32[2,32]{1,0:T(2,128)S(1)}, f32[2,32]{1,0:T(2,128)}, u32[]{:S(2)}) copy-start(f32[2,32]{1,0:T(2,128)} %charge_ref.1) | copy-start | bytes 772
  0.7 62.8 %copy-start.5 = (f32[2,32]{1,0:T(2,128)S(1)}, f32[2,32]{1,0:T(2,128)}, u32[]{:S(2)}) copy-start(f32[2,32]{1,0:T(2,128)} %spin_ref.1) | copy-start | bytes 772
  96.2 11.7 %collective-permute-start = (bf16[2,8,2,16,8,128]{5,4,3,2,1,0:T(8,128)(2,1)S(1)}, bf16[2,8,2,16,8,128]{5,4,3,2,1,0:T(8,128)(2,1)S(1)}, u32[]{:S(2)}, u32[]{:S(2)}) collective-permute-start(bf16[2,8,2,16,8,128]{5,4,3,2,1,0:T(8,128)(2,1)S(1)} %bitcast.12), channel_id=1, source_target_pairs={{0,1},{1,0},{2,3},{3,2},{4,5},{5,4},{6,7},{7,6},{8,9},{9,8},{10,11... | collective-permute-start | bytes 3145736 | tf_op jit(solution)/shard_map/ppermute | solution.py:389
